TPU v7x, 32 devices: a whole 2x2x4 slice. The times are simulated.
32 devices in a mesh: row: 4 (over y, x), col: 8 (over z, core).
Axes of the slice: x: 2, y: 2, z: 4, core: 2. Of those that a mesh axis runs over, the one named last changes fastest.
Arguments:
- history: bfloat16 [2, 4096, 4096], P(None, 'row', 'col'), may hold values from -2 to 2, as said below
- start_strip: float32 [2, 2048, 4096], P(None, 'col', 'row'), may hold values from -6 to 6
- coupling: float32 [32], replicated, may hold values from 0.5 to 1.5
- dyson_inverse: float32 [2, 2, 64, 64], replicated, may hold values from -3 to 3, as said below
Outputs:
- earlier: float32 [2, 2048, 4096], P(None, None, 'col')
- later: float32 [2, 2048, 4096], P(None, 'col', 'row')
Inputs may be any that keep to these rules, and one draw needn't show every extreme that they name: history is anti-Hermitian: its element at row (s, a), column (t, b) is minus the complex conjugate of its element at row (t, b), column (s, a). `dyson_inverse`: each group's inverse is lower triangular in time.
All inputs are finite; a program needn't handle non-finite values.
Results may differ from a plain program's by a relative error of at most 0.0043.
Values may be sent and summed in bfloat16 or wider, within the bound.
A program may use at most 192 MiB of HBM per device.

v0:
```python
import functools

import jax
import jax.numpy as jnp
from jax import lax
from jax.experimental import pallas as pl
from jax.experimental.pallas import tpu as pltpu
from jax.sharding import PartitionSpec as P

TIME_STEP = 0.15


def complex_product(first_pair, second_pair):
    real_out = jnp.dot(first_pair[0], second_pair[0], preferred_element_type=jnp.float32) - jnp.dot(
        first_pair[1], second_pair[1], preferred_element_type=jnp.float32
    )
    imag_out = jnp.dot(first_pair[0], second_pair[1], preferred_element_type=jnp.float32) + jnp.dot(
        first_pair[1], second_pair[0], preferred_element_type=jnp.float32
    )
    return jnp.stack([real_out, imag_out])


def mirror_product(sigma_pair, tile_pair):
    contract = (((1,), (1,)), ((), ()))
    real_real = lax.dot_general(
        sigma_pair[0], tile_pair[0], contract, preferred_element_type=jnp.float32
    )
    imag_imag = lax.dot_general(
        sigma_pair[1], tile_pair[1], contract, preferred_element_type=jnp.float32
    )
    real_imag = lax.dot_general(
        sigma_pair[0], tile_pair[1], contract, preferred_element_type=jnp.float32
    )
    imag_real = lax.dot_general(
        sigma_pair[1], tile_pair[0], contract, preferred_element_type=jnp.float32
    )
    return jnp.stack([-real_real - imag_imag, real_imag - imag_real])


def self_energy(green, row_weight, col_weight):
    magnitude = green[0] * green[0] + green[1] * green[1]
    factor = -(row_weight[:, None] * col_weight[None, :]) * magnitude
    return green * factor[None]


def orbital_weights(coupling, offset, count):
    orbitals = coupling.shape[0]
    position = (offset + jnp.arange(count, dtype=jnp.int32)) % orbitals
    one_hot = (position[:, None] == jnp.arange(orbitals, dtype=jnp.int32)[None, :]).astype(
        jnp.float32
    )
    return jnp.dot(
        one_hot, coupling, precision=lax.Precision.HIGHEST, preferred_element_type=jnp.float32
    )


MESH = pl.DeviceIdType.MESH
NN = (((1,), (0,)), ((), ()))
NT = (((1,), (1,)), ((), ()))


def mm(x, y, dims):
    return lax.dot_general(x, y, dims, preferred_element_type=jnp.float32)


def remote(src, dst, send_sem, recv_sem, row, col):
    return pltpu.make_async_remote_copy(
        src_ref=src,
        dst_ref=dst,
        send_sem=send_sem,
        recv_sem=recv_sem,
        device_id=(row, col),
        device_id_type=MESH,
    )


def entry_barrier(row, q, core, lines, rows):
    barrier = pltpu.get_barrier_semaphore()

    def greet(to_row, to_col):
        pl.semaphore_signal(barrier, inc=1, device_id=(to_row, to_col), device_id_type=MESH)

    greet(row, 2 * q + 1 - core)
    for k in range(1, rows):
        greet(lax.rem(row + k, rows), 2 * q + core)

    @pl.when(q > 0)
    def _():
        greet(row, 2 * (q - 1) + core)

    @pl.when(q < lines - 1)
    def _():
        greet(row, 2 * (q + 1) + core)

    ends = jnp.minimum(q, 1) + jnp.minimum(lines - 1 - q, 1)
    pl.semaphore_wait(barrier, rows + ends)


def first_kernel(lines, rows, sig, hist, out, blocks, parts, recv, local, hop_s, hop_r, pair_s, pair_r, sum_s, sum_r):
    row = lax.axis_index("row")
    col = lax.axis_index("col")
    q, core = lax.div(col, 2), lax.rem(col, 2)
    strip = sig.shape[1]
    share = out.shape[2]
    entry_barrier(row, q, core, lines, rows)

    own = pltpu.make_async_copy(sig, blocks.at[col], local)
    own.start()
    own.wait()

    def hop(way, s):
        step = 1 - 2 * way
        block = blocks.at[2 * (q - step * s) + core]
        return remote(block, block, hop_s.at[way, s], hop_r.at[way, s], row, 2 * (q + step) + core)

    def sends(way, s):
        if way == 0:
            return jnp.logical_and(q < lines - 1, q - s >= 0)
        return jnp.logical_and(q > 0, q + s <= lines - 1)

    def arrived(way, s):
        if way == 0:
            return q - 1 - s >= 0
        return q + 1 + s <= lines - 1

    def origin(way, s):
        step = 1 - 2 * way
        return q - step * (s + 1)

    def pair(line, at):
        block = blocks.at[2 * line + core]
        return remote(block, block, pair_s.at[at], pair_r.at[at], row, 2 * q + 1 - core)

    def spread(j, k):
        to = lax.rem(row + k, rows)
        return remote(
            parts.at[j, to], recv.at[j, k - 1], sum_s.at[j, k - 1], sum_r.at[j, k - 1], to, col
        )

    def compute(j):
        real = mm(blocks[j, 0], hist[0], NN) - mm(blocks[j, 1], hist[1], NN)
        imag = mm(blocks[j, 0], hist[1], NN) + mm(blocks[j, 1], hist[0], NN)
        at = pl.ds(pl.multiple_of(j * strip, strip), strip)
        for r in range(rows):
            cut = slice(r * share, (r + 1) * share)
            parts[j, r, 0] = real[:, cut].astype(jnp.bfloat16)
            parts[j, r, 1] = imag[:, cut].astype(jnp.bfloat16)

            @pl.when(row == r)
            def _():
                out[0, at, :] = real[:, cut]
                out[1, at, :] = imag[:, cut]

        for k in range(1, rows):
            spread(j, k).start()

    for way in (0, 1):

        @pl.when(sends(way, 0))
        def _():
            hop(way, 0).start()

    pair(q, 2 * (lines - 1)).start()

    def own_step(i, c):
        @pl.when(i == 1)
        def _():
            pair(q, 2 * (lines - 1)).wait_recv()

        compute(2 * q + core + i - 2 * core * i)
        return c

    lax.fori_loop(0, 2, own_step, 0)

    def step(s, c):
        for way in (0, 1):

            @pl.when(arrived(way, s))
            def _():
                hop(way, s).wait_recv()
                pair(origin(way, s), 2 * s + way).start()

            @pl.when(jnp.logical_and(s < lines - 2, sends(way, s + 1)))
            def _():
                hop(way, s + 1).start()

        def each(i, c2):
            way, other = lax.rem(i, 2), lax.div(i, 2)
            line = q - (1 - 2 * way) * (s + 1)

            @pl.when(jnp.logical_and(line >= 0, line <= lines - 1))
            def _():
                @pl.when(other == 1)
                def _():
                    pair(line, 2 * s + way).wait_recv()

                compute(2 * line + core + other - 2 * core * other)

            return c2

        lax.fori_loop(0, 4, each, 0)
        return c

    lax.fori_loop(0, lines - 1, step, 0)

    def finish(j, c):
        at = pl.ds(pl.multiple_of(j * strip, strip), strip)
        for k in range(1, rows):
            spread(j, k).wait_recv()
        for p in (0, 1):
            total = out[p, at, :]
            for k in range(1, rows):
                total += recv[j, k - 1, p].astype(jnp.float32)
            out[p, at, :] = total
        for k in range(1, rows):
            spread(j, k).wait_send()
        return c

    lax.fori_loop(0, 2 * lines, finish, 0)
    pair(q, 2 * (lines - 1)).wait_send()

    def drain(s, c):
        for way in (0, 1):

            @pl.when(sends(way, s))
            def _():
                hop(way, s).wait_send()

            @pl.when(arrived(way, s))
            def _():
                pair(origin(way, s), 2 * s + way).wait_send()

        return c

    lax.fori_loop(0, lines - 1, drain, 0)


def second_kernel(
    lines, rows, tau, near, hist, out, wide, taus, give, take, stage, land,
    local, pair_s, pair_r, hop_s, hop_r, tau_s, tau_r, wide_s, wide_r,
):
    row = lax.axis_index("row")
    col = lax.axis_index("col")
    q, core = lax.div(col, 2), lax.rem(col, 2)
    half = lax.div(2 * q, lines)
    strip = out.shape[1]
    entry_barrier(row, q, core, lines, rows)

    def span(j):
        return pl.ds(pl.multiple_of(j * strip, strip), strip)

    def spread(j, k):
        return remote(
            tau.at[:, span(j)],
            taus.at[row, :, span(j)],
            tau_s.at[j, k - 1],
            tau_r.at[j, k - 1],
            lax.rem(row + k, rows),
            col,
        )

    share = near.shape[2]
    mesh_2x2 = rows == 4
    beside = row + 1 - 2 * lax.rem(row, 2)
    across = lax.rem(row + 2, 4)
    direct = [beside, across] if mesh_2x2 else [lax.rem(row + k, rows) for k in range(1, rows)]

    def columns(r):
        return pl.ds(pl.multiple_of(r * share, share), share)

    mine = wide.at[:, :, columns(row)]

    def widen(k):
        return remote(near, mine, wide_s.at[k], wide_r.at[k], direct[k], col)

    def relay(k):
        block = wide.at[k, :, columns(direct[k])]
        return remote(block, block, wide_s.at[2 + k], wide_r.at[2 + k], direct[1 - k], col)

    def order(i):
        t, way = lax.div(i, 2), lax.rem(i + half, 2)
        d = (lines - 1 - t) * (1 - way) + t * way
        return d, way, (d - q) * (1 - 2 * way)

    def issue(d):
        for j in (2 * d + 1 - core, 2 * d + core):
            for k in range(1, rows):
                spread(j, k).start()

    def early(i, c):
        d, way, far = order(i)

        @pl.when(far > 0)
        def _():
            issue(d)

        return c

    lax.fori_loop(0, 2 * (lines - 1), early, 0)
    issue(q)
    for k in range(len(direct)):
        widen(k).start()
    own_wide = pltpu.make_async_copy(near, mine, local.at[0])
    own_wide.start()
    own_tau = pltpu.make_async_copy(tau, taus.at[row], local.at[1])
    own_tau.start()
    own_tau.wait()

    def product(j):
        for k in range(1, rows):
            spread(j, k).wait_recv()
        at = span(j)
        real_in = jnp.concatenate([taus[r, 0, at, :] for r in range(rows)], axis=1)
        imag_in = jnp.concatenate([taus[r, 1, at, :] for r in range(rows)], axis=1)
        real = -mm(real_in, hist[0], NT) - mm(imag_in, hist[1], NT)
        imag = mm(real_in, hist[1], NT) - mm(imag_in, hist[0], NT)
        return real, imag

    def pair(d):
        return remote(
            give.at[d], take.at[d], pair_s.at[d], pair_r.at[d], row, 2 * q + 1 - core
        )

    def hop(way, d):
        to = q + 1 - 2 * way
        return remote(
            stage.at[d], land.at[way, d], hop_s.at[d], hop_r.at[way, d], row, 2 * to + core
        )

    def offer(d):
        real, imag = product(2 * d + 1 - core)
        give[d, 0] = real.astype(jnp.bfloat16)
        give[d, 1] = imag.astype(jnp.bfloat16)
        pair(d).start()

    def gather(d):
        real, imag = product(2 * d + core)
        out[0] = real
        out[1] = imag
        pair(d).wait_recv()
        for p in (0, 1):
            out[p] += take[d, p].astype(jnp.float32)

    def add(way, d):
        hop(way, d).wait_recv()
        for p in (0, 1):
            out[p] += land[way, d, p].astype(jnp.float32)

    def step(i, c):
        d, way, far = order(i)

        @pl.when(far > 0)
        def _():
            offer(d)
            gather(d)

            @pl.when(jnp.logical_and(way == 0, q > 0))
            def _():
                add(0, d)

            @pl.when(jnp.logical_and(way == 1, q < lines - 1))
            def _():
                add(1, d)

            for p in (0, 1):
                stage[d, p] = out[p].astype(jnp.bfloat16)
            hop(way, d).start()

        return c

    lax.fori_loop(0, 2 * (lines - 1), step, 0)
    if mesh_2x2:
        for k in (0, 1):
            widen(k).wait_recv()
        for k in (0, 1):
            relay(k).start()
    offer(q)
    gather(q)

    @pl.when(q > 0)
    def _():
        add(0, q)

    @pl.when(q < lines - 1)
    def _():
        add(1, q)

    def drain(d, c):
        pair(d).wait_send()

        @pl.when(d > q)
        def _():
            hop(0, d).wait_send()

        @pl.when(d < q)
        def _():
            hop(1, d).wait_send()

        return c

    lax.fori_loop(0, lines, drain, 0)

    def drain_tau(j, c):
        for k in range(1, rows):
            spread(j, k).wait_send()
        return c

    lax.fori_loop(0, 2 * lines, drain_tau, 0)
    for k in range(len(direct)):
        widen(k).wait_send()
        if mesh_2x2:
            relay(k).wait()
        else:
            widen(k).wait_recv()
    own_wide.wait()


VMEM = pl.BlockSpec(memory_space=pltpu.VMEM)
DMA = pltpu.SemaphoreType.DMA


def first_sums(sigma, history, lines, rows):
    strip, depth = sigma.shape[1:]
    cols = 2 * lines
    share = history.shape[2] // rows
    bf16 = jnp.bfloat16
    return pl.pallas_call(
        functools.partial(first_kernel, lines, rows),
        out_shape=jax.ShapeDtypeStruct((2, strip * cols, share), jnp.float32),
        in_specs=[VMEM] * 2,
        out_specs=VMEM,
        scratch_shapes=[
            pltpu.VMEM((cols, 2, strip, depth), bf16),
            pltpu.VMEM((cols, rows, 2, strip, share), bf16),
            pltpu.VMEM((cols, rows - 1, 2, strip, share), bf16),
            DMA,
            DMA((2, lines - 1)),
            DMA((2, lines - 1)),
            DMA((2 * lines - 1,)),
            DMA((2 * lines - 1,)),
            DMA((cols, rows - 1)),
            DMA((cols, rows - 1)),
        ],
        compiler_params=pltpu.CompilerParams(
            collective_id=0, has_side_effects=True, vmem_limit_bytes=40 * 1024 * 1024
        ),
        name="first_sums",
    )(sigma, history)


def second_sums(tau, near, history, lines, rows):
    depth = history.shape[1]
    strip = tau.shape[1] // (2 * lines)
    bf16 = jnp.bfloat16
    return pl.pallas_call(
        functools.partial(second_kernel, lines, rows),
        out_shape=(
            jax.ShapeDtypeStruct((2, strip, depth), jnp.float32),
            jax.ShapeDtypeStruct(near.shape[:2] + (rows * near.shape[2],), bf16),
        ),
        in_specs=[VMEM] * 3,
        out_specs=(VMEM, pl.BlockSpec(memory_space=pl.ANY)),
        scratch_shapes=[
            pltpu.VMEM((rows,) + tau.shape, bf16),
            pltpu.VMEM((lines, 2, strip, depth), bf16),
            pltpu.VMEM((lines, 2, strip, depth), bf16),
            pltpu.VMEM((lines, 2, strip, depth), bf16),
            pltpu.VMEM((2, lines, 2, strip, depth), bf16),
            DMA((2,)),
            DMA((lines,)),
            DMA((lines,)),
            DMA((lines,)),
            DMA((2, lines)),
            DMA((2 * lines, rows - 1)),
            DMA((2 * lines, rows - 1)),
            DMA((max(rows - 1, 4),)),
            DMA((max(rows - 1, 4),)),
        ],
        compiler_params=pltpu.CompilerParams(
            collective_id=1, has_side_effects=True, vmem_limit_bytes=52 * 1024 * 1024
        ),
        name="second_sums",
    )(tau, near, history)


def stacked_dyson(inverse, source):
    group_len = inverse.shape[1]
    matrix = TIME_STEP * jnp.concatenate(
        [
            jnp.concatenate([inverse[0], -inverse[1]], axis=1),
            jnp.concatenate([inverse[1], inverse[0]], axis=1),
        ],
        axis=0,
    )
    flat = source.reshape(2 * group_len, -1)
    solved = jnp.dot(
        matrix, flat, precision=lax.Precision.HIGHEST, preferred_element_type=jnp.float32
    )
    return solved.reshape(source.shape)


def shards(history, start_strip, coupling, dyson_inverse):
    row_count = lax.axis_size("row")
    col_count = lax.axis_size("col")
    row_index = lax.axis_index("row")
    col_index = lax.axis_index("col")
    strip_rows = start_strip.shape[1]
    strip_cols = start_strip.shape[2]
    group_rows = strip_rows * col_count
    tile_cols = history.shape[2]
    share_cols = tile_cols // row_count
    sigma_first = self_energy(
        start_strip,
        orbital_weights(coupling, col_index * strip_rows, strip_rows),
        orbital_weights(coupling, row_index * strip_cols, strip_cols),
    ).astype(jnp.bfloat16)
    fits = share_cols % 128 == 0
    if fits:
        shares = first_sums(sigma_first, history, col_count // 2, row_count)
    else:
        partial_first = complex_product(
            lax.all_gather(sigma_first, "col", axis=1, tiled=True), history
        )
        shares = lax.psum_scatter(partial_first, "row", scatter_dimension=2, tiled=True)
    solved_part = stacked_dyson(dyson_inverse[0], shares)
    sigma_second = self_energy(
        solved_part,
        orbital_weights(coupling, 0, group_rows),
        orbital_weights(coupling, col_index * tile_cols + row_index * share_cols, share_cols),
    ).astype(jnp.bfloat16)
    solved_sigma = stacked_dyson(
        dyson_inverse[1], sigma_second.astype(jnp.float32)
    ).astype(jnp.bfloat16)
    if fits:
        later_strip, wide = second_sums(
            solved_sigma, solved_part.astype(jnp.bfloat16), history, col_count // 2, row_count
        )
        return (wide.astype(jnp.float32), later_strip)
    earlier = lax.all_gather(solved_part, "row", axis=2, tiled=True)
    tau = lax.all_gather(solved_sigma, "row", axis=2, tiled=True)
    partial_second = mirror_product(tau, history)
    later_strip = lax.psum_scatter(partial_second, "col", scatter_dimension=1, tiled=True)
    return (earlier, later_strip)


def solution(mesh):
    return jax.shard_map(
        shards,
        mesh=mesh,
        in_specs=(P(None, "row", "col"), P(None, "col", "row"), P(), P()),
        out_specs=(P(None, None, "col"), P(None, "col", "row")),
        check_vma=False,
    )
```

profile of v0, /device:TPU:9, one launch (start us, length us, event | category | flops | bytes accessed | tf_op | source)
XLA Modules:
  0.0 217.8 jit_solution(4454967567926858095)
XLA Ops:
  0.6 0.0 copy-start
  0.6 0.0 copy-start.2
  0.7 0.6 copy-done
  1.3 0.2 convolution_bitcast_fusion
  1.5 0.1 and_select_fusion.1
  1.6 0.2 fusion.5
  1.8 0.1 add_select_fusion.1
  1.8 0.4 fusion.3
  2.3 0.7 fusion.1
  3.0 0.8 fusion.40
  3.8 0.8 slice_bitcast_fusion.2
  4.6 1.8 multiply_bitcast_fusion
  6.4 0.0 copy-done.2
  6.4 0.0 copy-start.1
  6.4 0.4 multiply_convert_fusion.1.sig
  6.8 1.2 copy-done.1
  8.0 70.8 %first_sums.1 = f32[2,2048,128]{2,1,0:T(8,128)S(1)} custom-call(bf16[2,256,1024]{2,1,0:T(8,128)(2,1)S(1)} %multiply_convert_fusion.1.sig, bf16[2,1024,512]{2,1,0:T(8,128)(2,1)S(1)} %copy-done.1), custom_call_target="tpu_custom_call" | custom-call | tf_op jit(solution)/shard_map/first_sums/pallas_call | solution.py:427
  78.8 1.5 reshape.168
  80.3 3.5 %fusion.42 = (bf16[128,4096]{1,0:T(8,128)(2,1)S(1)}, f32[128,4096]{1,0:T(8,128)S(1)}) fusion(f32[128,4096]{1,0:T(8,128)} %reshape.168, f32[64,64]{1,0:T(8,128)S(1)} %get-tuple-element.11, f32[64,64]{1,0:T(8,128)S(1)} %get-tuple-element.10, f32[64,64]{1,0:T(8,128)S(1)} %get-tuple-element.7), kind=kOutput, calls=%fused_computation.71 | convolution fusion | flops 805896192 | bytes 5292032 | tf_op jit(solution)/shard_map/dot_general | solution.py:496
  83.8 1.3 convert_element_type.30.near
  85.1 0.1 fusion
  85.3 1.1 add.100
  86.4 1.6 negate_multiply_fusion
  88.0 1.5 mul.132
  89.4 2.7 %mul.133 = f32[128,4096]{1,0:T(8,128)} reshape(f32[2,2048,128]{2,1,0:T(8,128)} %mul.132) | data formatting | bytes 4194304 | tf_op jit(solution)/shard_map/mul | solution.py:43
  92.1 2.7 %convolution_convert_fusion = bf16[128,4096]{1,0:T(8,128)(2,1)S(1)} fusion(f32[128,4096]{1,0:T(8,128)S(1)} %get-tuple-element.13, f32[128,4096]{1,0:T(8,128)} %mul.133, f32[64,64]{1,0:T(8,128)S(1)} %get-tuple-element.9, f32[64,64]{1,0:T(8,128)S(1)} %get-tuple-element.8, f32[64,64]{1,0:T(8,128)S(1)} %get-tuple-element.6), kind=kOutput, calls=%fused_computation | convolution fusion | flops 806944768 | bytes 5292032 | tf_op jit(solution)/shard_map/dot_general | solution.py:496
  94.9 0.5 convert_element_type.28.tau
  95.4 114.1 %second_sums.1 = (f32[2,256,1024]{2,1,0:T(8,128)}, bf16[2,2048,512]{2,1,0:T(8,128)(2,1)}) custom-call(bf16[2,2048,128]{2,1,0:T(8,128)(2,1)S(1)} %convert_element_type.28.tau, bf16[2,2048,128]{2,1,0:T(8,128)(2,1)} %convert_element_type.30.near, bf16[2,1024,512]{2,1,0:T(8,128)(2,1)} %hist.3), custom_call_target="tpu_custom_call" | custom-call | tf_op jit(solution)/shard_map/second_sums/pallas_call | solution.py:455
  209.5 0.0 copy-start.3
  209.5 6.9 %convert_element_type.31 = f32[2,2048,512]{2,1,0:T(8,128)} convert(bf16[2,2048,512]{2,1,0:T(8,128)(2,1)} %get-tuple-element.4) | non-fusion elementwise | flops 2097152 | bytes 12582912 | tf_op jit(solution)/shard_map/convert_element_type | solution.py:538
  216.4 0.0 copy-done.3
  216.4 1.3 copy.7
  (2 shorter events, 0.0 us)
Async XLA Ops:
  0.6 0.7 copy-start
  0.6 5.8 %copy-start.2 = (f32[2,256,1024]{2,1,0:T(8,128)S(1)}, f32[2,256,1024]{2,1,0:T(8,128)}, u32[]{:S(2)}) copy-start(f32[2,256,1024]{2,1,0:T(8,128)} %param.5) | copy-start | bytes 6291460
  6.4 1.6 copy-start.1
  209.5 6.9 %copy-start.3 = (f32[2,256,1024]{2,1,0:T(8,128)S(1)}, f32[2,256,1024]{2,1,0:T(8,128)}, u32[]{:S(2)}) copy-start(f32[2,256,1024]{2,1,0:T(8,128)} %get-tuple-element.17) | copy-start | bytes 6291460
where the time goes:
time: 218 us
  Pallas kernels  185 us (85%)
  local copies, waits for them, and re-layouts  12.7 us (6%)
  other arithmetic  11.7 us (5%)
  matrix products  7.78 us (4%)
    pallas_call x1, Pallas kernels, second_sums(): pl.pallas_call(functools.partial(second_kernel, lines, rows), out_shape=(...  114 us
    pallas_call x1, Pallas kernels, first_sums(): pl.pallas_call(functools.partial(first_kernel, lines, rows), out_shape=ja...  70.8 us
    convert_element_type x1, other arithmetic, shards(): return (wide.astype(jnp.float32), later_strip)  6.93 us
    dot_general x2, matrix products, stacked_dyson(): jnp.dot(matrix, flat, precision=lax.Precision.HIGHEST, preferred_element_...  6.22 us

commit v1 on v0

v1 whole, which is shorter than its diff:
```python
import functools

import jax
import jax.numpy as jnp
from jax import lax
from jax.experimental import pallas as pl
from jax.experimental.pallas import tpu as pltpu
from jax.sharding import PartitionSpec as P

TIME_STEP = 0.15


def complex_product(first_pair, second_pair):
    real_out = jnp.dot(first_pair[0], second_pair[0], preferred_element_type=jnp.float32) - jnp.dot(
        first_pair[1], second_pair[1], preferred_element_type=jnp.float32
    )
    imag_out = jnp.dot(first_pair[0], second_pair[1], preferred_element_type=jnp.float32) + jnp.dot(
        first_pair[1], second_pair[0], preferred_element_type=jnp.float32
    )
    return jnp.stack([real_out, imag_out])


def mirror_product(sigma_pair, tile_pair):
    contract = (((1,), (1,)), ((), ()))
    real_real = lax.dot_general(
        sigma_pair[0], tile_pair[0], contract, preferred_element_type=jnp.float32
    )
    imag_imag = lax.dot_general(
        sigma_pair[1], tile_pair[1], contract, preferred_element_type=jnp.float32
    )
    real_imag = lax.dot_general(
        sigma_pair[0], tile_pair[1], contract, preferred_element_type=jnp.float32
    )
    imag_real = lax.dot_general(
        sigma_pair[1], tile_pair[0], contract, preferred_element_type=jnp.float32
    )
    return jnp.stack([-real_real - imag_imag, real_imag - imag_real])


def self_energy(green, row_weight, col_weight):
    magnitude = green[0] * green[0] + green[1] * green[1]
    factor = -(row_weight[:, None] * col_weight[None, :]) * magnitude
    return green * factor[None]


def orbital_weights(coupling, offset, count):
    orbitals = coupling.shape[0]
    position = (offset + jnp.arange(count, dtype=jnp.int32)) % orbitals
    one_hot = (position[:, None] == jnp.arange(orbitals, dtype=jnp.int32)[None, :]).astype(
        jnp.float32
    )
    return jnp.dot(
        one_hot, coupling, precision=lax.Precision.HIGHEST, preferred_element_type=jnp.float32
    )


MESH = pl.DeviceIdType.MESH
NN = (((1,), (0,)), ((), ()))
NT = (((1,), (1,)), ((), ()))
CHUNKS = 4
(
    RELAY,
    PRODUCT,
    SOLVE,
    UPDATE,
    SPREAD_TAU,
    GIVE,
    KEEP,
    CHAIN,
    SEND_NEAR,
    RELAY_NEAR,
    NOTHING,
) = range(11)


def mm(x, y, dims):
    return lax.dot_general(x, y, dims, preferred_element_type=jnp.float32)


def remote(src, dst, send_sem, recv_sem, row, col):
    return pltpu.make_async_remote_copy(
        src_ref=src,
        dst_ref=dst,
        send_sem=send_sem,
        recv_sem=recv_sem,
        device_id=(row, col),
        device_id_type=MESH,
    )


def head_start(q, lines):
    return CHUNKS if q == 0 else min(q, CHUNKS)


COST = {
    RELAY: 0.15,
    PRODUCT: 2.2,
    SOLVE: 1.3,
    UPDATE: 2.3,
    SPREAD_TAU: 0.15,
    GIVE: 2.4,
    KEEP: 3.0,
    CHAIN: 0.5,
    SEND_NEAR: 0.1,
    RELAY_NEAR: 0.1,
}
RANK = {
    RELAY: 0,
    SPREAD_TAU: 1,
    CHAIN: 2,
    SOLVE: 3,
    PRODUCT: 4,
    KEEP: 4.5,
    GIVE: 5,
    UPDATE: 6,
    SEND_NEAR: 7,
    RELAY_NEAR: 7,
}
HOP, PLANE_SUM, PLANE_TAU, LATENCY = 22.5, 5.6, 2.8, 1.5


def plan(lines):
    last = lines - 1
    arrive, links, plane = {}, {}, [0.0] * lines
    todo, done, clock, order = [], [{} for _ in range(lines)], [0.0] * lines, []

    def hop(q, to, time, event):
        begin = max(time, links.get((q, to), 0.0))
        links[(q, to)] = begin + HOP / CHUNKS
        arrive[(to,) + event] = begin + HOP / CHUNKS + LATENCY

    def share(q, time, length, event):
        begin = max(time, plane[q])
        plane[q] = begin + length
        arrive[(q,) + event] = begin + length + LATENCY

    for q in range(lines):
        tasks = set()
        for m in range(lines):
            tasks |= {(PRODUCT, m, 0), (PRODUCT, m, 1)}
            for j in (2 * m, 2 * m + 1):
                tasks |= {(SOLVE, j, 0), (SPREAD_TAU, j, 0)}
            tasks |= {(kind, m, 0) for kind in (GIVE, KEEP, SEND_NEAR, RELAY_NEAR)}
            tasks |= {(UPDATE, m, later) for later in range(m + 1, lines)}
            if m != q:
                tasks |= {(RELAY, m, k) for k in range(CHUNKS)}
                if not ((m < q and q == last) or (m > q and q == 0)):
                    tasks |= {(CHAIN, m, k) for k in range(CHUNKS)}
        if q > 0:
            tasks |= {(CHAIN, q, k) for k in range(CHUNKS)}
        if q < last:
            tasks |= {(CHAIN, q, CHUNKS + k) for k in range(CHUNKS)}
        todo.append(tasks)
        order.append([])
        arrive[(q, "pair", q)] = 3.0
        if q > 0:
            for k in range(CHUNKS):
                hop(q, q - 1, 0.0, ("block", q, k))
        if q < last:
            for k in range(head_start(q, lines)):
                hop(q, q + 1, 0.0, ("block", q, k))

    def ready(q, task):
        kind, a, b = task
        mine = done[q]

        def got(*event):
            return arrive.get((q,) + event)

        if kind == RELAY:
            need = [got("block", a, b)]
        elif kind == PRODUCT and b == 1:
            need = [got("pair", a)]
        elif kind == PRODUCT:
            need = [0.0] if a == q else [mine.get((RELAY, a, k)) for k in range(CHUNKS)]
        elif kind == SOLVE:
            m = a // 2
            need = [got("sum", m, 0), got("sum", m, 1)]
            need += [mine.get((UPDATE, x, m)) for x in range(m)]
            need += [mine.get((SOLVE, a - 1, 0))] if a else []
        elif kind == UPDATE:
            need = [mine.get((SOLVE, 2 * a + 1, 0))]
        elif kind == SPREAD_TAU:
            need = [got("tau", a)]
        elif kind == GIVE:
            need = [got("all", 2 * a), got("all", 2 * a + 1)]
        elif kind == KEEP:
            need = [mine.get((GIVE, a, 0))]
        elif kind == CHAIN:
            need = [mine.get((KEEP, a, 0)), got("part", a, b)]
        elif kind == SEND_NEAR:
            need = [mine.get((SOLVE, 2 * a + 1, 0)), plane[q]]
        else:
            need = [got("near", a)]
        return None if None in need else max(need)

    def rank(q, task):
        kind, a, b = task
        extra = 0.1 * a - 0.5 * (a == q) if kind == PRODUCT else 0.1 * b * (kind == UPDATE)
        return RANK[kind] + extra

    while any(todo):
        best = None
        for q in range(lines):
            able = []
            for task in todo[q]:
                time = ready(q, task)
                if time is not None:
                    able.append((max(time, clock[q]), rank(q, task), task))
            if able:
                first = min(able)
                if best is None or first[0] < best[0]:
                    best = (first[0], q, first[2])
        begin, q, task = best
        kind, a, b = task
        todo[q].remove(task)
        end = begin + COST[kind]
        if kind == KEEP:
            end = max(end, arrive[(q, "give", a)] + 0.6)
        done[q][task] = end
        clock[q] = end
        order[q].append(task)
        side = q + 1 if a > q else q - 1
        if kind == RELAY:
            to = q + 1 if a < q else q - 1
            if 0 <= to <= last:
                hop(q, to, begin, ("block", a, b))
            if b == CHUNKS - 1:
                arrive[(q, "pair", a)] = end + 2.0
                if a == q - 1 and q < last:
                    for k in range(head_start(q, lines), CHUNKS):
                        hop(q, q + 1, end, ("block", q, k))
        elif kind == PRODUCT:
            share(q, end, PLANE_SUM, ("sum", a, b))
        elif kind == SOLVE:
            share(q, end, PLANE_TAU, ("tau", a))
        elif kind == SPREAD_TAU:
            share(q, end, PLANE_TAU / 2, ("all", a))
        elif kind == SEND_NEAR:
            share(q, end, 2 * PLANE_TAU, ("near", a))
        elif kind == RELAY_NEAR:
            share(q, end, PLANE_TAU, ("wide", a))
        elif kind == GIVE:
            arrive[(q, "give", a)] = end + 3.0
        elif a != q and (kind == CHAIN or (kind == KEEP and q == (last if a < q else 0))):
            for k in [b] if kind == CHAIN else range(CHUNKS):
                slot = CHUNKS + k if side == a and a < q else k
                hop(q, side, end, ("part", a, slot))
    return order


def step_words(lines):
    order = plan(lines)
    longest = max(len(steps) for steps in order)
    longest += -longest % 3
    packed = []
    for steps in order:
        codes = [kind * 64 + a * 8 + b for kind, a, b in steps]
        codes += [NOTHING * 64] * (longest - len(codes))
        packed.append(
            [
                codes[i] + 1024 * codes[i + 1] + 1024 * 1024 * codes[i + 2]
                for i in range(0, longest, 3)
            ]
        )
    return longest, packed


def entry_barrier(row, q, core, lines, rows, wait):
    barrier = pltpu.get_barrier_semaphore()
    ends = jnp.minimum(q, 1) + jnp.minimum(lines - 1 - q, 1)
    if wait:
        pl.semaphore_wait(barrier, rows + ends)
        return

    def greet(to_row, to_col):
        pl.semaphore_signal(barrier, inc=1, device_id=(to_row, to_col), device_id_type=MESH)

    greet(row, 2 * q + 1 - core)
    for k in range(1, rows):
        greet(lax.rem(row + k, rows), 2 * q + core)

    @pl.when(q > 0)
    def _():
        greet(row, 2 * (q - 1) + core)

    @pl.when(q < lines - 1)
    def _():
        greet(row, 2 * (q + 1) + core)


def fused_kernel(
    lines, rows, count, packed, strip, hist, weight, dyson, later, wide,
    blocks, parts, recv, own, new, tau, source, near, taus, give, take, stage, land, held,
    hop_s, hop_r, pair_s, pair_r, sum_s, sum_r, tau_s, tau_r, near_s, near_r, local,
    give_s, give_r, chain_s, chain_r,
):
    row = lax.axis_index("row")
    col = lax.axis_index("col")
    q, core = lax.div(col, 2), lax.rem(col, 2)
    last = lines - 1
    height, depth = strip.shape[1:]
    share = near.shape[2]
    orbitals = weight.shape[0]
    times = height // orbitals
    total = times * 2 * lines
    piece = height // CHUNKS
    beside = row + 1 - 2 * lax.rem(row, 2)
    across = lax.rem(row + 2, 4)
    direct = [beside, across]
    bf16 = jnp.bfloat16

    def span(j):
        return pl.ds(pl.multiple_of(j * height, height), height)

    def double(m):
        return pl.ds(pl.multiple_of(2 * m * height, 2 * height), 2 * height)

    def cut(k):
        return pl.ds(pl.multiple_of(k * piece, piece), piece)

    def columns(r):
        return pl.ds(pl.multiple_of(r * share, share), share)

    def slab(n):
        return pl.ds(pl.multiple_of(n * orbitals, orbitals), orbitals)

    def hop(way, m, k):
        block = blocks.at[2 * m + core, :, cut(k)]
        to = 2 * (q + 1 - 2 * way) + core
        return remote(block, block, hop_s.at[way, m, k], hop_r.at[m, k], row, to)

    def pair(m, k):
        block = blocks.at[2 * m + core, :, cut(k)]
        return remote(block, block, pair_s.at[m, k], pair_r.at[m, k], row, 2 * q + 1 - core)

    def spread(j, k):
        to = lax.rem(row + k, rows)
        return remote(
            parts.at[j, to], recv.at[j, k - 1], sum_s.at[j, k - 1], sum_r.at[j, k - 1], to, col
        )

    def send_tau(j, k):
        block = taus.at[row, :, span(j)]
        return remote(block, block, tau_s.at[j, k], tau_r.at[j, k], direct[k], col)

    def relay_tau(j, k):
        block = taus.at[direct[k], k, span(j)]
        return remote(block, block, tau_s.at[j, 2 + k], tau_r.at[j, 2 + k], direct[1 - k], col)

    def send_near(m, k):
        return remote(
            near.at[:, double(m)],
            wide.at[:, double(m), columns(row)],
            near_s.at[m, k],
            near_r.at[m, k],
            direct[k],
            col,
        )

    def relay_near(m, k):
        block = wide.at[k, double(m), columns(direct[k])]
        return remote(block, block, near_s.at[m, 2 + k], near_r.at[m, 2 + k], direct[1 - k], col)

    def own_near(m):
        return pltpu.make_async_copy(
            near.at[:, double(m)], wide.at[:, double(m), columns(row)], local.at[m]
        )

    def swap(d):
        return remote(give.at[d], take.at[d], give_s.at[d], give_r.at[d], row, 2 * q + 1 - core)

    def chain(way, d, k):
        to = q + 1 - 2 * way
        slot = jnp.where(jnp.logical_and(d == to, way == 1), lines, d)
        return remote(
            stage.at[d, :, cut(k)],
            land.at[slot, :, cut(k)],
            chain_s.at[d, k],
            chain_r.at[slot, k],
            row,
            2 * to + core,
        )

    def chain_on(d, k):
        @pl.when(d > q)
        def _():
            chain(0, d, k).start()

        @pl.when(d < q)
        def _():
            chain(1, d, k).start()

    def update(acc, src, group, low, n, j):
        def add(i, c):
            at = low + i
            real, imag = acc[0, slab(at), :], acc[1, slab(at), :]
            for t in range(times):
                m = j * times + t
                there = (2 * group * total + at) * total + m
                dr, di = dyson[there], dyson[there + total * total]
                sr, si = src[0, slab(m), :], src[1, slab(m), :]
                real += dr * sr - di * si
                imag += dr * si + di * sr
            acc[0, slab(at), :] = real
            acc[1, slab(at), :] = imag
            return c

        lax.fori_loop(0, n, add, 0)

    def op_relay(m, k):
        hop(0, m, k).wait_recv()

        @pl.when(jnp.logical_and(m < q, q < last))
        def _():
            hop(0, m, k).start()

        @pl.when(jnp.logical_and(m > q, q > 0))
        def _():
            hop(1, m, k).start()

        pair(m, k).start()

        @pl.when(jnp.logical_and(m == q - 1, k == CHUNKS - 1))
        def _():
            rest()

    def rest():
        for x in range(CHUNKS):

            @pl.when(jnp.logical_and(q < last, jnp.logical_and(q > 0, x >= q)))
            def _():
                hop(0, q, x).start()

    def op_product(m, other):
        @pl.when(other == 1)
        def _():
            for k in range(CHUNKS):
                pair(m, k).wait_recv()

        j = 2 * m + core + other - 2 * core * other
        real = mm(blocks[j, 0], hist[0], NN) - mm(blocks[j, 1], hist[1], NN)
        imag = mm(blocks[j, 0], hist[1], NN) + mm(blocks[j, 1], hist[0], NN)
        for r in range(rows):
            part = slice(r * share, (r + 1) * share)
            parts[j, r, 0] = real[:, part].astype(bf16)
            parts[j, r, 1] = imag[:, part].astype(bf16)

            @pl.when(row == r)
            def _():
                own[0, span(j), :] = real[:, part]
                own[1, span(j), :] = imag[:, part]

        for k in range(1, rows):
            spread(j, k).start()

    def op_solve(j):
        at = span(j)
        for k in range(1, rows):
            spread(j, k).wait_recv()
        for p in (0, 1):
            value = own[p, at, :]
            for k in range(1, rows):
                value += recv[j, k - 1, p].astype(jnp.float32)
            own[p, at, :] = TIME_STEP * value

        @pl.when(lax.rem(j, 2) == 1)
        def _():
            update(new, own, 0, j * times, times, j - 1)

        update(new, own, 0, j * times, times, j)

        def sigma(i, c):
            rows_at = slab(j * times + i)
            real, imag = new[0, rows_at, :], new[1, rows_at, :]
            near[0, rows_at, :] = real.astype(bf16)
            near[1, rows_at, :] = imag.astype(bf16)
            factor = weight[...] * (real * real + imag * imag)
            source[0, rows_at, :] = TIME_STEP * (real * factor).astype(bf16).astype(jnp.float32)
            source[1, rows_at, :] = TIME_STEP * (imag * factor).astype(bf16).astype(jnp.float32)
            return c

        lax.fori_loop(0, times, sigma, 0)

        @pl.when(lax.rem(j, 2) == 1)
        def _():
            update(tau, source, 1, j * times, times, j - 1)

        update(tau, source, 1, j * times, times, j)
        for p in (0, 1):
            taus[row, p, at, :] = tau[p, at, :].astype(bf16)
        for k in (0, 1):
            send_tau(j, k).start()

    def op_update(m, later_m):
        def both(half, c):
            update(new, own, 0, 2 * times * later_m, 2 * times, 2 * m + half)
            update(tau, source, 1, 2 * times * later_m, 2 * times, 2 * m + half)
            return c

        lax.fori_loop(0, 2, both, 0)

    def op_spread_tau(j):
        for k in (0, 1):
            send_tau(j, k).wait_recv()
        for k in (0, 1):
            relay_tau(j, k).start()

    def second(j):
        for k in (0, 1):
            relay_tau(j, k).wait_recv()
        at = span(j)
        real_in = jnp.concatenate([taus[r, 0, at, :] for r in range(rows)], axis=1)
        imag_in = jnp.concatenate([taus[r, 1, at, :] for r in range(rows)], axis=1)
        real = -mm(real_in, hist[0], NT) - mm(imag_in, hist[1], NT)
        imag = mm(real_in, hist[1], NT) - mm(imag_in, hist[0], NT)
        return real, imag

    def held_at(d):
        return d - jnp.where(d > q, 1, 0)

    def op_second(d, keep):
        pair_sums = second(2 * d + core + (1 - keep) * (1 - 2 * core))

        @pl.when(keep == 0)
        def _():
            for p in (0, 1):
                give[d, p] = pair_sums[p].astype(bf16)
            swap(d).start()

        @pl.when(keep == 1)
        def _():
            swap(d).wait_recv()
            begins = jnp.logical_or(
                jnp.logical_and(d < q, q == last), jnp.logical_and(d > q, q == 0)
            )

            @pl.when(d == q)
            def _():
                for p in (0, 1):
                    later[p] = pair_sums[p] + take[d, p].astype(jnp.float32)

            @pl.when(begins)
            def _():
                for p in (0, 1):
                    value = pair_sums[p] + take[d, p].astype(jnp.float32)
                    stage[d, p] = value.astype(bf16)
                for k in range(CHUNKS):
                    chain_on(d, k)

            @pl.when(jnp.logical_and(d != q, jnp.logical_not(begins)))
            def _():
                for p in (0, 1):
                    held[held_at(d), p] = pair_sums[p] + take[d, p].astype(jnp.float32)

    def op_chain(d, b):
        way, k = lax.div(b, CHUNKS), lax.rem(b, CHUNKS)
        at = cut(k)
        slot = jnp.where(way == 1, lines, d)
        pltpu.make_async_remote_copy(
            src_ref=stage.at[d, :, at],
            dst_ref=land.at[slot, :, at],
            send_sem=chain_s.at[d, k],
            recv_sem=chain_r.at[slot, k],
            device_id=(row, 2 * q + 1 - core),
            device_id_type=MESH,
        ).wait_recv()

        @pl.when(d == q)
        def _():
            for p in (0, 1):
                later[p, at, :] += land[slot, p, at, :].astype(jnp.float32)

        @pl.when(d != q)
        def _():
            for p in (0, 1):
                value = held[held_at(d), p, at, :] + land[slot, p, at, :].astype(jnp.float32)
                stage[d, p, at, :] = value.astype(bf16)
            chain_on(d, k)

    def op_send_near(m):
        own_near(m).start()
        for k in (0, 1):
            send_near(m, k).start()

    def op_relay_near(m):
        for k in (0, 1):
            send_near(m, k).wait_recv()
        for k in (0, 1):
            relay_near(m, k).start()

    entry_barrier(row, q, core, lines, rows, False)

    def fill(i, c):
        at = slab(i)
        scale = jnp.concatenate([weight[...]] * (depth // weight.shape[1]), axis=1)
        real, imag = strip[0, at, :], strip[1, at, :]
        factor = scale * (real * real + imag * imag)
        blocks[col, 0, at, :] = (real * factor).astype(bf16)
        blocks[col, 1, at, :] = (imag * factor).astype(bf16)
        return c

    lax.fori_loop(0, times, fill, 0)
    entry_barrier(row, q, core, lines, rows, True)

    for x in range(CHUNKS):

        @pl.when(jnp.logical_and(q < last, jnp.logical_or(q == 0, x < q)))
        def _():
            hop(0, q, x).start()

    for x in range(CHUNKS):

        @pl.when(q > 0)
        def _():
            hop(1, q, x).start()

    for x in range(CHUNKS):
        pair(q, x).start()

    def clear(n, c):
        for p in (0, 1):
            new[p, slab(n), :] = jnp.zeros((orbitals, share), jnp.float32)
            tau[p, slab(n), :] = jnp.zeros((orbitals, share), jnp.float32)
        return c

    lax.fori_loop(0, total, clear, 0)

    words = []
    for w in range(count // 3):
        word = jnp.int32(packed[last][w])
        for x in range(last):
            word = jnp.where(q == x, jnp.int32(packed[x][w]), word)
        words.append(word)

    def step(i, c):
        which, place = lax.div(i, 3), lax.rem(i, 3)
        word = words[0]
        for w in range(1, len(words)):
            word = jnp.where(which == w, words[w], word)
        middle = lax.rem(lax.div(word, 1024), 1024)
        code = jnp.where(place == 1, middle, lax.rem(word, 1024))
        code = jnp.where(place == 2, lax.div(word, 1024 * 1024), code)
        kind, a, b = lax.div(code, 64), lax.rem(lax.div(code, 8), 8), lax.rem(code, 8)

        @pl.when(kind == RELAY)
        def _():
            op_relay(a, b)

        @pl.when(kind == PRODUCT)
        def _():
            op_product(a, b)

        @pl.when(kind == SOLVE)
        def _():
            op_solve(a)

        @pl.when(kind == UPDATE)
        def _():
            op_update(a, b)

        @pl.when(kind == SPREAD_TAU)
        def _():
            op_spread_tau(a)

        @pl.when(jnp.logical_or(kind == GIVE, kind == KEEP))
        def _():
            op_second(a, kind - GIVE)

        @pl.when(kind == CHAIN)
        def _():
            op_chain(a, b)

        @pl.when(kind == SEND_NEAR)
        def _():
            op_send_near(a)

        @pl.when(kind == RELAY_NEAR)
        def _():
            op_relay_near(a)

        return c

    lax.fori_loop(0, count, step, 0)

    def drain_line(m, c):
        for k in range(CHUNKS):

            @pl.when(jnp.logical_and(m <= q, q < last))
            def _():
                hop(0, m, k).wait_send()

            @pl.when(jnp.logical_and(m >= q, q > 0))
            def _():
                hop(1, m, k).wait_send()

            pair(m, k).wait_send()

            @pl.when(m != q)
            def _():
                chain(0, m, k).wait_send()

        swap(m).wait_send()
        own_near(m).wait()
        for k in (0, 1):
            send_near(m, k).wait_send()
            relay_near(m, k).wait()
        return c

    lax.fori_loop(0, lines, drain_line, 0)

    def drain_block(j, c):
        for k in range(1, rows):
            spread(j, k).wait_send()
        for k in (0, 1):
            send_tau(j, k).wait_send()
            relay_tau(j, k).wait_send()
        return c

    lax.fori_loop(0, 2 * lines, drain_block, 0)


VMEM = pl.BlockSpec(memory_space=pltpu.VMEM)
DMA = pltpu.SemaphoreType.DMA


def fused(strip, history, weight, dyson, lines, rows):
    height, depth = strip.shape[1:]
    width = history.shape[2]
    share = width // rows
    blocks = 2 * lines
    full = blocks * height
    count, packed = step_words(lines)
    bf16, f32 = jnp.bfloat16, jnp.float32
    return pl.pallas_call(
        functools.partial(fused_kernel, lines, rows, count, packed),
        out_shape=(
            jax.ShapeDtypeStruct(strip.shape, f32),
            jax.ShapeDtypeStruct((2, full, width), bf16),
        ),
        in_specs=[VMEM, VMEM, VMEM, pl.BlockSpec(memory_space=pltpu.SMEM)],
        out_specs=(VMEM, pl.BlockSpec(memory_space=pl.ANY)),
        scratch_shapes=[
            pltpu.VMEM((blocks, 2, height, depth), bf16),
            pltpu.VMEM((blocks, rows, 2, height, share), bf16),
            pltpu.VMEM((blocks, rows - 1, 2, height, share), bf16),
            pltpu.VMEM((2, full, share), f32),
            pltpu.VMEM((2, full, share), f32),
            pltpu.VMEM((2, full, share), f32),
            pltpu.VMEM((2, full, share), f32),
            pltpu.VMEM((2, full, share), bf16),
            pltpu.VMEM((rows, 2, full, share), bf16),
            pltpu.VMEM((lines, 2, height, depth), bf16),
            pltpu.VMEM((lines, 2, height, depth), bf16),
            pltpu.VMEM((lines, 2, height, depth), bf16),
            pltpu.VMEM((lines + 1, 2, height, depth), bf16),
            pltpu.VMEM((lines - 1, 2, height, depth), f32),
            DMA((2, lines, CHUNKS)),
            DMA((lines, CHUNKS)),
            DMA((lines, CHUNKS)),
            DMA((lines, CHUNKS)),
            DMA((blocks, rows - 1)),
            DMA((blocks, rows - 1)),
            DMA((blocks, 4)),
            DMA((blocks, 4)),
            DMA((lines, 4)),
            DMA((lines, 4)),
            DMA((lines,)),
            DMA((lines,)),
            DMA((lines,)),
            DMA((lines, CHUNKS)),
            DMA((lines + 1, CHUNKS)),
        ],
        compiler_params=pltpu.CompilerParams(
            collective_id=0, has_side_effects=True, vmem_limit_bytes=63 * 1024 * 1024
        ),
        name="group_updates",
    )(strip, history, weight, dyson)


def stacked_dyson(inverse, source):
    group_len = inverse.shape[1]
    matrix = TIME_STEP * jnp.concatenate(
        [
            jnp.concatenate([inverse[0], -inverse[1]], axis=1),
            jnp.concatenate([inverse[1], inverse[0]], axis=1),
        ],
        axis=0,
    )
    flat = source.reshape(2 * group_len, -1)
    solved = jnp.dot(
        matrix, flat, precision=lax.Precision.HIGHEST, preferred_element_type=jnp.float32
    )
    return solved.reshape(source.shape)


def shards(history, start_strip, coupling, dyson_inverse):
    row_count = lax.axis_size("row")
    col_count = lax.axis_size("col")
    row_index = lax.axis_index("row")
    col_index = lax.axis_index("col")
    strip_rows = start_strip.shape[1]
    strip_cols = start_strip.shape[2]
    group_rows = strip_rows * col_count
    tile_cols = history.shape[2]
    share_cols = tile_cols // row_count
    orbitals = coupling.shape[0]
    fits = (
        row_count == 4
        and col_count <= 8
        and share_cols == 128
        and share_cols % orbitals == 0
        and strip_rows % (16 * CHUNKS) == 0
        and strip_rows % orbitals == 0
        and group_rows // orbitals == dyson_inverse.shape[2]
    )
    if fits:
        weight = -(coupling[:, None] * jnp.tile(coupling, share_cols // orbitals)[None, :])
        later_strip, wide = fused(
            start_strip, history, weight, dyson_inverse.reshape(-1), col_count // 2, row_count
        )
        return (wide.astype(jnp.float32), later_strip)
    sigma_first = self_energy(
        start_strip,
        orbital_weights(coupling, col_index * strip_rows, strip_rows),
        orbital_weights(coupling, row_index * strip_cols, strip_cols),
    ).astype(jnp.bfloat16)
    partial_first = complex_product(
        lax.all_gather(sigma_first, "col", axis=1, tiled=True), history
    )
    shares = lax.psum_scatter(partial_first, "row", scatter_dimension=2, tiled=True)
    solved_part = stacked_dyson(dyson_inverse[0], shares)
    sigma_second = self_energy(
        solved_part,
        orbital_weights(coupling, 0, group_rows),
        orbital_weights(coupling, col_index * tile_cols + row_index * share_cols, share_cols),
    ).astype(jnp.bfloat16)
    solved_sigma = stacked_dyson(
        dyson_inverse[1], sigma_second.astype(jnp.float32)
    ).astype(jnp.bfloat16)
    earlier = lax.all_gather(solved_part, "row", axis=2, tiled=True)
    tau = lax.all_gather(solved_sigma, "row", axis=2, tiled=True)
    partial_second = mirror_product(tau, history)
    later_strip = lax.psum_scatter(partial_second, "col", scatter_dimension=1, tiled=True)
    return (earlier, later_strip)


def solution(mesh):
    return jax.shard_map(
        shards,
        mesh=mesh,
        in_specs=(P(None, "row", "col"), P(None, "col", "row"), P(), P()),
        out_specs=(P(None, None, "col"), P(None, "col", "row")),
        check_vma=False,
    )
```

time: 218 us -> 181 us (0.83)
  the two profiles are of different devices: /device:TPU:9 before, /device:TPU:27 now
where the time goes in v1:
time: 181 us; the launch traced here: 180 us
  Pallas kernels  168 us (93%)
  other arithmetic  8.27 us (5%)
  local copies, waits for them, and re-layouts  3.68 us (2%)
    pallas_call x1, Pallas kernels, fused(): pl.pallas_call(functools.partial(fused_kernel, lines, rows, count, packed...  168 us
    convert_element_type x1, other arithmetic, shards(): return (wide.astype(jnp.float32), later_strip)  6.93 us

profile of v1, /device:TPU:27, one launch (start us, length us, event | category | flops | bytes accessed | tf_op | source)
XLA Modules:
  0.0 180.4 jit_solution(500566307773229313)
XLA Ops:
  0.6 0.7 tile.2
  1.3 0.1 mul.16
  1.4 1.3 multiply_negate_fusion.weight
  2.7 1.6 reshape.10.dyson
  4.3 167.9 %group_updates.1 = (f32[2,256,1024]{2,1,0:T(8,128)}, bf16[2,2048,512]{2,1,0:T(8,128)(2,1)}) custom-call(f32[2,256,1024]{2,1,0:T(8,128)} %strip.1, bf16[2,1024,512]{2,1,0:T(8,128)(2,1)} %hist.1, f32[32,128]{1,0:T(8,128)} %multiply_negate_fusion.weight, f32[16384]{0:T(1024)} %reshape.10.dyson), custom_call_target="tpu_custom_call" | custom-call | tf_op jit(solution)/shard_map/group_updates/pallas_call | solution.py:735
  172.2 0.0 copy-start
  172.2 6.9 %convert_element_type.3 = f32[2,2048,512]{2,1,0:T(8,128)} convert(bf16[2,2048,512]{2,1,0:T(8,128)(2,1)} %get-tuple-element.4) | non-fusion elementwise | flops 2097152 | bytes 12582912 | tf_op jit(solution)/shard_map/convert_element_type | solution.py:822
  179.1 0.0 copy-done
  179.1 1.3 copy.7
Async XLA Ops:
  172.2 6.9 %copy-start = (f32[2,256,1024]{2,1,0:T(8,128)S(1)}, f32[2,256,1024]{2,1,0:T(8,128)}, u32[]{:S(2)}) copy-start(f32[2,256,1024]{2,1,0:T(8,128)} %get-tuple-element.9) | copy-start | bytes 6291460

commit v2 on v1

--- a/solution.py
+++ b/solution.py
@@ -58,6 +58,7 @@
 NN = (((1,), (0,)), ((), ()))
 NT = (((1,), (1,)), ((), ()))
 CHUNKS = 4
+HEAD = 4
 (
     RELAY,
     PRODUCT,
@@ -69,8 +70,9 @@
     CHAIN,
     SEND_NEAR,
     RELAY_NEAR,
+    JOIN,
     NOTHING,
-) = range(11)
+) = range(12)
 
 
 def mm(x, y, dims):
@@ -88,181 +90,50 @@
     )
 
 
-def head_start(q, lines):
-    return CHUNKS if q == 0 else min(q, CHUNKS)
-
-
-COST = {
-    RELAY: 0.15,
-    PRODUCT: 2.2,
-    SOLVE: 1.3,
-    UPDATE: 2.3,
-    SPREAD_TAU: 0.15,
-    GIVE: 2.4,
-    KEEP: 3.0,
-    CHAIN: 0.5,
-    SEND_NEAR: 0.1,
-    RELAY_NEAR: 0.1,
+ORDERS = {
+    4: (
+        (
+            128, 129, 1280, 1281, 256, 272, 18, 1024, 17, 386, 16, 19, 144, 145,
+            385, 1296, 32, 1297, 288, 304, 544, 35, 402, 560, 34, 33, 161, 656,
+            160, 784, 1313, 1312, 51, 403, 320, 336, 50, 387, 576, 48, 49, 592,
+            176, 177, 672, 1328, 800, 1329, 419, 528, 352, 368, 608, 624, 1072, 1056,
+            688, 1152, 816, 1040, 512, 640, 1168, 768, 900, 901, 1184, 903, 1200, 902,
+        ),
+        (
+            0, 145, 144, 32, 1, 2, 34, 35, 1296, 3, 33, 129, 128, 1280,
+            160, 1281, 1297, 50, 161, 256, 51, 272, 385, 288, 48, 1313, 304, 1312,
+            49, 177, 512, 402, 386, 528, 176, 320, 336, 576, 1329, 544, 419, 592,
+            640, 1040, 1328, 403, 560, 672, 387, 800, 928, 768, 352, 368, 608, 930,
+            624, 896, 1072, 1168, 656, 931, 688, 816, 899, 944, 945, 784, 1056, 897,
+            898, 946, 1024, 914, 913, 916, 1200, 915, 947, 1152, 918, 912, 929, 1184,
+            919, 917,
+        ),
+        (
+            16, 160, 0, 50, 1, 49, 51, 161, 2, 3, 1313, 48, 128, 17,
+            129, 176, 1312, 18, 1281, 1280, 177, 19, 256, 145, 144, 272, 512, 387,
+            386, 528, 1296, 1329, 1297, 385, 1328, 640, 288, 304, 402, 320, 560, 336,
+            403, 768, 896, 419, 576, 544, 897, 352, 368, 899, 898, 608, 592, 656,
+            624, 1040, 784, 688, 1072, 912, 672, 1024, 1056, 913, 816, 1168, 914, 944,
+            945, 915, 800, 946, 1152, 930, 1184, 928, 931, 1200, 947, 932, 934, 933,
+            929, 935,
+        ),
+        (
+            16, 0, 176, 32, 2, 1328, 1, 177, 3, 128, 129, 1280, 17, 1281,
+            1329, 256, 18, 272, 386, 512, 19, 528, 144, 33, 34, 145, 640, 35,
+            1296, 160, 768, 1297, 161, 385, 288, 304, 1312, 544, 402, 560, 1313, 1040,
+            656, 320, 784, 336, 387, 1024, 592, 576, 1056, 419, 403, 352, 672, 368,
+            1168, 800, 624, 608, 1072, 1184, 688, 1152, 816, 1200, 944, 946, 945, 947,
+        ),
+    ),
 }
-RANK = {
-    RELAY: 0,
-    SPREAD_TAU: 1,
-    CHAIN: 2,
-    SOLVE: 3,
-    PRODUCT: 4,
-    KEEP: 4.5,
-    GIVE: 5,
-    UPDATE: 6,
-    SEND_NEAR: 7,
-    RELAY_NEAR: 7,
-}
-HOP, PLANE_SUM, PLANE_TAU, LATENCY = 22.5, 5.6, 2.8, 1.5
-
-
-def plan(lines):
-    last = lines - 1
-    arrive, links, plane = {}, {}, [0.0] * lines
-    todo, done, clock, order = [], [{} for _ in range(lines)], [0.0] * lines, []
-
-    def hop(q, to, time, event):
-        begin = max(time, links.get((q, to), 0.0))
-        links[(q, to)] = begin + HOP / CHUNKS
-        arrive[(to,) + event] = begin + HOP / CHUNKS + LATENCY
-
-    def share(q, time, length, event):
-        begin = max(time, plane[q])
-        plane[q] = begin + length
-        arrive[(q,) + event] = begin + length + LATENCY
-
-    for q in range(lines):
-        tasks = set()
-        for m in range(lines):
-            tasks |= {(PRODUCT, m, 0), (PRODUCT, m, 1)}
-            for j in (2 * m, 2 * m + 1):
-                tasks |= {(SOLVE, j, 0), (SPREAD_TAU, j, 0)}
-            tasks |= {(kind, m, 0) for kind in (GIVE, KEEP, SEND_NEAR, RELAY_NEAR)}
-            tasks |= {(UPDATE, m, later) for later in range(m + 1, lines)}
-            if m != q:
-                tasks |= {(RELAY, m, k) for k in range(CHUNKS)}
-                if not ((m < q and q == last) or (m > q and q == 0)):
-                    tasks |= {(CHAIN, m, k) for k in range(CHUNKS)}
-        if q > 0:
-            tasks |= {(CHAIN, q, k) for k in range(CHUNKS)}
-        if q < last:
-            tasks |= {(CHAIN, q, CHUNKS + k) for k in range(CHUNKS)}
-        todo.append(tasks)
-        order.append([])
-        arrive[(q, "pair", q)] = 3.0
-        if q > 0:
-            for k in range(CHUNKS):
-                hop(q, q - 1, 0.0, ("block", q, k))
-        if q < last:
-            for k in range(head_start(q, lines)):
-                hop(q, q + 1, 0.0, ("block", q, k))
-
-    def ready(q, task):
-        kind, a, b = task
-        mine = done[q]
-
-        def got(*event):
-            return arrive.get((q,) + event)
-
-        if kind == RELAY:
-            need = [got("block", a, b)]
-        elif kind == PRODUCT and b == 1:
-            need = [got("pair", a)]
-        elif kind == PRODUCT:
-            need = [0.0] if a == q else [mine.get((RELAY, a, k)) for k in range(CHUNKS)]
-        elif kind == SOLVE:
-            m = a // 2
-            need = [got("sum", m, 0), got("sum", m, 1)]
-            need += [mine.get((UPDATE, x, m)) for x in range(m)]
-            need += [mine.get((SOLVE, a - 1, 0))] if a else []
-        elif kind == UPDATE:
-            need = [mine.get((SOLVE, 2 * a + 1, 0))]
-        elif kind == SPREAD_TAU:
-            need = [got("tau", a)]
-        elif kind == GIVE:
-            need = [got("all", 2 * a), got("all", 2 * a + 1)]
-        elif kind == KEEP:
-            need = [mine.get((GIVE, a, 0))]
-        elif kind == CHAIN:
-            need = [mine.get((KEEP, a, 0)), got("part", a, b)]
-        elif kind == SEND_NEAR:
-            need = [mine.get((SOLVE, 2 * a + 1, 0)), plane[q]]
-        else:
-            need = [got("near", a)]
-        return None if None in need else max(need)
-
-    def rank(q, task):
-        kind, a, b = task
-        extra = 0.1 * a - 0.5 * (a == q) if kind == PRODUCT else 0.1 * b * (kind == UPDATE)
-        return RANK[kind] + extra
-
-    while any(todo):
-        best = None
-        for q in range(lines):
-            able = []
-            for task in todo[q]:
-                time = ready(q, task)
-                if time is not None:
-                    able.append((max(time, clock[q]), rank(q, task), task))
-            if able:
-                first = min(able)
-                if best is None or first[0] < best[0]:
-                    best = (first[0], q, first[2])
-        begin, q, task = best
-        kind, a, b = task
-        todo[q].remove(task)
-        end = begin + COST[kind]
-        if kind == KEEP:
-            end = max(end, arrive[(q, "give", a)] + 0.6)
-        done[q][task] = end
-        clock[q] = end
-        order[q].append(task)
-        side = q + 1 if a > q else q - 1
-        if kind == RELAY:
-            to = q + 1 if a < q else q - 1
-            if 0 <= to <= last:
-                hop(q, to, begin, ("block", a, b))
-            if b == CHUNKS - 1:
-                arrive[(q, "pair", a)] = end + 2.0
-                if a == q - 1 and q < last:
-                    for k in range(head_start(q, lines), CHUNKS):
-                        hop(q, q + 1, end, ("block", q, k))
-        elif kind == PRODUCT:
-            share(q, end, PLANE_SUM, ("sum", a, b))
-        elif kind == SOLVE:
-            share(q, end, PLANE_TAU, ("tau", a))
-        elif kind == SPREAD_TAU:
-            share(q, end, PLANE_TAU / 2, ("all", a))
-        elif kind == SEND_NEAR:
-            share(q, end, 2 * PLANE_TAU, ("near", a))
-        elif kind == RELAY_NEAR:
-            share(q, end, PLANE_TAU, ("wide", a))
-        elif kind == GIVE:
-            arrive[(q, "give", a)] = end + 3.0
-        elif a != q and (kind == CHAIN or (kind == KEEP and q == (last if a < q else 0))):
-            for k in [b] if kind == CHAIN else range(CHUNKS):
-                slot = CHUNKS + k if side == a and a < q else k
-                hop(q, side, end, ("part", a, slot))
-    return order
-
 
 def step_words(lines):
-    order = plan(lines)
-    longest = max(len(steps) for steps in order)
-    longest += -longest % 3
+    longest = max(len(steps) for steps in ORDERS[lines])
+    longest += longest % 2
     packed = []
-    for steps in order:
-        codes = [kind * 64 + a * 8 + b for kind, a, b in steps]
-        codes += [NOTHING * 64] * (longest - len(codes))
-        packed.append(
-            [
-                codes[i] + 1024 * codes[i + 1] + 1024 * 1024 * codes[i + 2]
-                for i in range(0, longest, 3)
-            ]
-        )
+    for steps in ORDERS[lines]:
+        codes = list(steps) + [NOTHING * 128] * (longest - len(steps))
+        packed.append([codes[i] + 2048 * codes[i + 1] for i in range(0, longest, 2)])
     return longest, packed
 
 
@@ -290,8 +161,9 @@
 
 
 def fused_kernel(
-    lines, rows, count, packed, strip, hist, weight, dyson, later, wide,
-    blocks, parts, recv, own, new, tau, source, near, taus, give, take, stage, land, held,
+    lines, rows, count, packed, strip, history, coupling, dyson, later_out, wide,
+    later, hist, weight, blocks, parts, first, keep, sums, joined, own, new, tau, source, near, taus,
+    give, take, stage, land, held,
     hop_s, hop_r, pair_s, pair_r, sum_s, sum_r, tau_s, tau_r, near_s, near_r, local,
     give_s, give_r, chain_s, chain_r,
 ):
@@ -299,8 +171,8 @@
     col = lax.axis_index("col")
     q, core = lax.div(col, 2), lax.rem(col, 2)
     last = lines - 1
-    height, depth = strip.shape[1:]
-    share = near.shape[2]
+    height, depth = later.shape[1:]
+    share = own.shape[2]
     orbitals = weight.shape[0]
     times = height // orbitals
     total = times * 2 * lines
@@ -310,6 +182,9 @@
     direct = [beside, across]
     bf16 = jnp.bfloat16
 
+    def head_start(at):
+        return lax.div(at * CHUNKS, HEAD)
+
     def span(j):
         return pl.ds(pl.multiple_of(j * height, height), height)
 
@@ -334,10 +209,15 @@
         block = blocks.at[2 * m + core, :, cut(k)]
         return remote(block, block, pair_s.at[m, k], pair_r.at[m, k], row, 2 * q + 1 - core)
 
-    def spread(j, k):
-        to = lax.rem(row + k, rows)
+    def send_parts(j, k):
         return remote(
-            parts.at[j, to], recv.at[j, k - 1], sum_s.at[j, k - 1], sum_r.at[j, k - 1], to, col
+            parts.at[j, k], first.at[j, k], sum_s.at[j, k], sum_r.at[j, k], direct[k], col
+        )
+
+    def send_joined(j, k):
+        return remote(
+            sums.at[j, k], joined.at[j, k], sum_s.at[j, 2 + k], sum_r.at[j, 2 + k],
+            direct[1 - k], col,
         )
 
     def send_tau(j, k):
@@ -397,9 +277,9 @@
             real, imag = acc[0, slab(at), :], acc[1, slab(at), :]
             for t in range(times):
                 m = j * times + t
-                there = (2 * group * total + at) * total + m
-                dr, di = dyson[there], dyson[there + total * total]
-                sr, si = src[0, slab(m), :], src[1, slab(m), :]
+                dr, di = dyson[group, 0, at, m], dyson[group, 1, at, m]
+                sr = src[0, slab(m), :].astype(jnp.float32)
+                si = src[1, slab(m), :].astype(jnp.float32)
                 real += dr * sr - di * si
                 imag += dr * si + di * sr
             acc[0, slab(at), :] = real
@@ -428,7 +308,7 @@
     def rest():
         for x in range(CHUNKS):
 
-            @pl.when(jnp.logical_and(q < last, jnp.logical_and(q > 0, x >= q)))
+            @pl.when(jnp.logical_and(q < last, jnp.logical_and(q > 0, x >= head_start(q))))
             def _():
                 hop(0, q, x).start()
 
@@ -442,27 +322,38 @@
         real = mm(blocks[j, 0], hist[0], NN) - mm(blocks[j, 1], hist[1], NN)
         imag = mm(blocks[j, 0], hist[1], NN) + mm(blocks[j, 1], hist[0], NN)
         for r in range(rows):
-            part = slice(r * share, (r + 1) * share)
-            parts[j, r, 0] = real[:, part].astype(bf16)
-            parts[j, r, 1] = imag[:, part].astype(bf16)
 
             @pl.when(row == r)
             def _():
-                own[0, span(j), :] = real[:, part]
-                own[1, span(j), :] = imag[:, part]
-
-        for k in range(1, rows):
-            spread(j, k).start()
+                mine, near_x, near_y, far = [
+                    slice(x * share, (x + 1) * share) for x in (r, r ^ 1, r ^ 2, r ^ 3)
+                ]
+                parts[j, 0, 0] = real[:, near_x].astype(bf16)
+                parts[j, 0, 1] = real[:, far].astype(bf16)
+                parts[j, 1, 0] = imag[:, near_y].astype(bf16)
+                parts[j, 1, 1] = imag[:, far].astype(bf16)
+                keep[j, 0] = real[:, near_y]
+                keep[j, 1] = imag[:, near_x]
+                own[0, span(j), :] = real[:, mine]
+                own[1, span(j), :] = imag[:, mine]
+
+        for k in (0, 1):
+            send_parts(j, k).start()
+
+    def op_join(m, other):
+        j = 2 * m + core + other - 2 * core * other
+        for k in (0, 1):
+            send_parts(j, k).wait_recv()
+            sums[j, k] = (keep[j, k] + first[j, k, 1].astype(jnp.float32)).astype(bf16)
+        for k in (0, 1):
+            send_joined(j, k).start()
 
     def op_solve(j):
         at = span(j)
-        for k in range(1, rows):
-            spread(j, k).wait_recv()
         for p in (0, 1):
-            value = own[p, at, :]
-            for k in range(1, rows):
-                value += recv[j, k - 1, p].astype(jnp.float32)
-            own[p, at, :] = TIME_STEP * value
+            send_joined(j, p).wait_recv()
+            others = first[j, p, 0].astype(jnp.float32) + joined[j, p].astype(jnp.float32)
+            own[p, at, :] = TIME_STEP * (own[p, at, :] + others)
 
         @pl.when(lax.rem(j, 2) == 1)
         def _():
@@ -476,8 +367,8 @@
             near[0, rows_at, :] = real.astype(bf16)
             near[1, rows_at, :] = imag.astype(bf16)
             factor = weight[...] * (real * real + imag * imag)
-            source[0, rows_at, :] = TIME_STEP * (real * factor).astype(bf16).astype(jnp.float32)
-            source[1, rows_at, :] = TIME_STEP * (imag * factor).astype(bf16).astype(jnp.float32)
+            source[0, rows_at, :] = (real * factor).astype(bf16)
+            source[1, rows_at, :] = (imag * factor).astype(bf16)
             return c
 
         lax.fori_loop(0, times, sigma, 0)
@@ -488,7 +379,7 @@
 
         update(tau, source, 1, j * times, times, j)
         for p in (0, 1):
-            taus[row, p, at, :] = tau[p, at, :].astype(bf16)
+            taus[row, p, at, :] = (TIME_STEP * tau[p, at, :]).astype(bf16)
         for k in (0, 1):
             send_tau(j, k).start()
 
@@ -589,12 +480,25 @@
         for k in (0, 1):
             relay_near(m, k).start()
 
+    load_hist = pltpu.make_async_copy(history, hist, local.at[lines])
+    load_strip = pltpu.make_async_copy(strip, later, local.at[lines + 1])
+    load_strip.start()
+    load_hist.start()
     entry_barrier(row, q, core, lines, rows, False)
+    place_row = lax.broadcasted_iota(jnp.int32, (orbitals, share), 0)
+    place_col = lax.rem(lax.broadcasted_iota(jnp.int32, (orbitals, share), 1), orbitals)
+    down = jnp.zeros((orbitals, share), jnp.float32)
+    along = jnp.zeros((orbitals, share), jnp.float32)
+    for a in range(orbitals):
+        down = jnp.where(place_row == a, coupling[a], down)
+        along = jnp.where(place_col == a, coupling[a], along)
+    weight[...] = -(down * along)
+    load_strip.wait()
 
     def fill(i, c):
         at = slab(i)
-        scale = jnp.concatenate([weight[...]] * (depth // weight.shape[1]), axis=1)
-        real, imag = strip[0, at, :], strip[1, at, :]
+        scale = jnp.concatenate([weight[...]] * (depth // share), axis=1)
+        real, imag = later[0, at, :], later[1, at, :]
         factor = scale * (real * real + imag * imag)
         blocks[col, 0, at, :] = (real * factor).astype(bf16)
         blocks[col, 1, at, :] = (imag * factor).astype(bf16)
@@ -605,7 +509,7 @@
 
     for x in range(CHUNKS):
 
-        @pl.when(jnp.logical_and(q < last, jnp.logical_or(q == 0, x < q)))
+        @pl.when(jnp.logical_and(q < last, jnp.logical_or(q == 0, x < head_start(q))))
         def _():
             hop(0, q, x).start()
 
@@ -625,23 +529,22 @@
         return c
 
     lax.fori_loop(0, total, clear, 0)
+    load_hist.wait()
 
     words = []
-    for w in range(count // 3):
+    for w in range(count // 2):
         word = jnp.int32(packed[last][w])
         for x in range(last):
             word = jnp.where(q == x, jnp.int32(packed[x][w]), word)
         words.append(word)
 
     def step(i, c):
-        which, place = lax.div(i, 3), lax.rem(i, 3)
+        which, place = lax.div(i, 2), lax.rem(i, 2)
         word = words[0]
         for w in range(1, len(words)):
             word = jnp.where(which == w, words[w], word)
-        middle = lax.rem(lax.div(word, 1024), 1024)
-        code = jnp.where(place == 1, middle, lax.rem(word, 1024))
-        code = jnp.where(place == 2, lax.div(word, 1024 * 1024), code)
-        kind, a, b = lax.div(code, 64), lax.rem(lax.div(code, 8), 8), lax.rem(code, 8)
+        code = jnp.where(place == 1, lax.div(word, 2048), lax.rem(word, 2048))
+        kind, a, b = lax.div(code, 128), lax.rem(lax.div(code, 16), 8), lax.rem(code, 16)
 
         @pl.when(kind == RELAY)
         def _():
@@ -651,6 +554,10 @@
         def _():
             op_product(a, b)
 
+        @pl.when(kind == JOIN)
+        def _():
+            op_join(a, b)
+
         @pl.when(kind == SOLVE)
         def _():
             op_solve(a)
@@ -682,6 +589,8 @@
         return c
 
     lax.fori_loop(0, count, step, 0)
+    leave = pltpu.make_async_copy(later, later_out, local.at[lines])
+    leave.start()
 
     def drain_line(m, c):
         for k in range(CHUNKS):
@@ -710,21 +619,24 @@
     lax.fori_loop(0, lines, drain_line, 0)
 
     def drain_block(j, c):
-        for k in range(1, rows):
-            spread(j, k).wait_send()
-        for k in (0, 1):
+        for k in (0, 1):
+            send_parts(j, k).wait_send()
+            send_joined(j, k).wait_send()
             send_tau(j, k).wait_send()
             relay_tau(j, k).wait_send()
         return c
 
     lax.fori_loop(0, 2 * lines, drain_block, 0)
+    leave.wait()
 
 
 VMEM = pl.BlockSpec(memory_space=pltpu.VMEM)
+ANY = pl.BlockSpec(memory_space=pl.ANY)
+SMEM = pl.BlockSpec(memory_space=pltpu.SMEM)
 DMA = pltpu.SemaphoreType.DMA
 
 
-def fused(strip, history, weight, dyson, lines, rows):
+def fused(strip, history, coupling, dyson, lines, rows):
     height, depth = strip.shape[1:]
     width = history.shape[2]
     share = width // rows
@@ -738,16 +650,22 @@
             jax.ShapeDtypeStruct(strip.shape, f32),
             jax.ShapeDtypeStruct((2, full, width), bf16),
         ),
-        in_specs=[VMEM, VMEM, VMEM, pl.BlockSpec(memory_space=pltpu.SMEM)],
-        out_specs=(VMEM, pl.BlockSpec(memory_space=pl.ANY)),
+        in_specs=[ANY, ANY, SMEM, SMEM],
+        out_specs=(ANY, ANY),
         scratch_shapes=[
+            pltpu.VMEM(strip.shape, f32),
+            pltpu.VMEM(history.shape, bf16),
+            pltpu.VMEM((coupling.shape[0], share), f32),
             pltpu.VMEM((blocks, 2, height, depth), bf16),
-            pltpu.VMEM((blocks, rows, 2, height, share), bf16),
-            pltpu.VMEM((blocks, rows - 1, 2, height, share), bf16),
+            pltpu.VMEM((blocks, 2, 2, height, share), bf16),
+            pltpu.VMEM((blocks, 2, 2, height, share), bf16),
+            pltpu.VMEM((blocks, 2, height, share), f32),
+            pltpu.VMEM((blocks, 2, height, share), bf16),
+            pltpu.VMEM((blocks, 2, height, share), bf16),
             pltpu.VMEM((2, full, share), f32),
             pltpu.VMEM((2, full, share), f32),
             pltpu.VMEM((2, full, share), f32),
-            pltpu.VMEM((2, full, share), f32),
+            pltpu.VMEM((2, full, share), bf16),
             pltpu.VMEM((2, full, share), bf16),
             pltpu.VMEM((rows, 2, full, share), bf16),
             pltpu.VMEM((lines, 2, height, depth), bf16),
@@ -759,13 +677,13 @@
             DMA((lines, CHUNKS)),
             DMA((lines, CHUNKS)),
             DMA((lines, CHUNKS)),
-            DMA((blocks, rows - 1)),
-            DMA((blocks, rows - 1)),
+            DMA((blocks, 4)),
+            DMA((blocks, 4)),
             DMA((blocks, 4)),
             DMA((blocks, 4)),
             DMA((lines, 4)),
             DMA((lines, 4)),
-            DMA((lines,)),
+            DMA((lines + 2,)),
             DMA((lines,)),
             DMA((lines,)),
             DMA((lines, CHUNKS)),
@@ -775,7 +693,56 @@
             collective_id=0, has_side_effects=True, vmem_limit_bytes=63 * 1024 * 1024
         ),
         name="group_updates",
-    )(strip, history, weight, dyson)
+    )(strip, history, coupling, dyson)
+
+
+def widen_kernel(pieces, wide, later, out, later_out, rough, fine, passing, in_s, out_s, pass_s):
+    size = wide.shape[1] // pieces
+
+    def fetch(i):
+        return pltpu.make_async_copy(wide.at[:, pl.ds(i * size, size)], rough.at[i], in_s.at[i])
+
+    def put(i):
+        return pltpu.make_async_copy(fine.at[i], out.at[:, pl.ds(i * size, size)], out_s.at[i])
+
+    take = pltpu.make_async_copy(later, passing, pass_s.at[0])
+    leave = pltpu.make_async_copy(passing, later_out, pass_s.at[1])
+    for i in range(pieces):
+        fetch(i).start()
+    take.start()
+    for i in range(pieces):
+        fetch(i).wait()
+        fine[i] = rough[i].astype(jnp.float32)
+        put(i).start()
+    take.wait()
+    leave.start()
+    for i in range(pieces):
+        put(i).wait()
+    leave.wait()
+
+
+def widen(wide, later):
+    pieces = 8
+    piece = (pieces, 2, wide.shape[1] // pieces, wide.shape[2])
+    return pl.pallas_call(
+        functools.partial(widen_kernel, pieces),
+        out_shape=(
+            jax.ShapeDtypeStruct(wide.shape, jnp.float32),
+            jax.ShapeDtypeStruct(later.shape, jnp.float32),
+        ),
+        in_specs=[ANY, ANY],
+        out_specs=(ANY, ANY),
+        scratch_shapes=[
+            pltpu.VMEM(piece, jnp.bfloat16),
+            pltpu.VMEM(piece, jnp.float32),
+            pltpu.VMEM(later.shape, jnp.float32),
+            DMA((pieces,)),
+            DMA((pieces,)),
+            DMA((2,)),
+        ],
+        compiler_params=pltpu.CompilerParams(vmem_limit_bytes=60 * 1024 * 1024),
+        name="widen",
+    )(wide, later)
 
 
 def stacked_dyson(inverse, source):
@@ -807,7 +774,8 @@
     orbitals = coupling.shape[0]
     fits = (
         row_count == 4
-        and col_count <= 8
+        and col_count // 2 in ORDERS
+        and col_count % 2 == 0
         and share_cols == 128
         and share_cols % orbitals == 0
         and strip_rows % (16 * CHUNKS) == 0
@@ -815,11 +783,10 @@
         and group_rows // orbitals == dyson_inverse.shape[2]
     )
     if fits:
-        weight = -(coupling[:, None] * jnp.tile(coupling, share_cols // orbitals)[None, :])
         later_strip, wide = fused(
-            start_strip, history, weight, dyson_inverse.reshape(-1), col_count // 2, row_count
+            start_strip, history, coupling, dyson_inverse, col_count // 2, row_count
         )
-        return (wide.astype(jnp.float32), later_strip)
+        return widen(wide, later_strip)
     sigma_first = self_energy(
         start_strip,
         orbital_weights(coupling, col_index * strip_rows, strip_rows),

time: 181 us -> 161 us (0.89)
  other arithmetic: 8.27 us -> 0 us
  Pallas kernels: 168 us -> 160 us
  local copies, waits for them, and re-layouts: 3.68 us -> 0 us
    pallas_call x1, Pallas kernels: 168 us -> 154 us  [fused(): pl.pallas_call(functools.partial(fused_kernel, lines, rows, count, packed...]
    convert_element_type x1 -> x0, other arithmetic: 6.93 us -> none  [shards(): return (wide.astype(jnp.float32), later_strip)]
    pallas_call x0 -> x1, Pallas kernels: none -> 6.18 us  [widen(): pl.pallas_call(functools.partial(widen_kernel, pieces), out_shape=(jax.Sh...]
where the time goes in v2:
time: 161 us
  Pallas kernels  160 us (99%)
    pallas_call x1, Pallas kernels, fused(): pl.pallas_call(functools.partial(fused_kernel, lines, rows, count, packed...  154 us
    pallas_call x1, Pallas kernels, widen(): pl.pallas_call(functools.partial(widen_kernel, pieces), out_shape=(jax.Sh...  6.18 us

profile of v2, /device:TPU:27, one launch (start us, length us, event | category | flops | bytes accessed | tf_op | source)
XLA Modules:
  0.0 160.7 jit_solution(10371799453427724128)
XLA Ops:
  0.6 153.9 %group_updates.1 = (f32[2,256,1024]{2,1,0:T(8,128)}, bf16[2,2048,512]{2,1,0:T(8,128)(2,1)}) custom-call(f32[2,256,1024]{2,1,0:T(8,128)} %strip.1, bf16[2,1024,512]{2,1,0:T(8,128)(2,1)} %history.1, f32[32]{0:T(128)} %coupling.1, f32[2,2,64,64]{3,2,1,0:T(8,128)} %dyson.1), custom_call_target="tpu_custom_call" | custom-call | tf_op jit(solution)/shard_map/group_updates/pallas_call | solution.py:647
  154.5 6.2 %widen.1 = (f32[2,2048,512]{2,1,0:T(8,128)}, f32[2,256,1024]{2,1,0:T(8,128)}) custom-call(bf16[2,2048,512]{2,1,0:T(8,128)(2,1)} %get-tuple-element.4.wide, f32[2,256,1024]{2,1,0:T(8,128)} %get-tuple-element.5.later), custom_call_target="tpu_custom_call" | custom-call | tf_op jit(solution)/shard_map/widen/pallas_call | solution.py:727

commit v3 on v2

--- a/solution.py
+++ b/solution.py
@@ -97,7 +97,7 @@
             385, 1296, 32, 1297, 288, 304, 544, 35, 402, 560, 34, 33, 161, 656,
             160, 784, 1313, 1312, 51, 403, 320, 336, 50, 387, 576, 48, 49, 592,
             176, 177, 672, 1328, 800, 1329, 419, 528, 352, 368, 608, 624, 1072, 1056,
-            688, 1152, 816, 1040, 512, 640, 1168, 768, 900, 901, 1184, 903, 1200, 902,
+            688, 1152, 816, 1040, 512, 640, 1168, 768, 908, 909, 1184, 911, 1200, 910,
         ),
         (
             0, 145, 144, 32, 1, 2, 34, 35, 1296, 3, 33, 129, 128, 1280,
@@ -105,8 +105,8 @@
             49, 177, 512, 402, 386, 528, 176, 320, 336, 576, 1329, 544, 419, 592,
             640, 1040, 1328, 403, 560, 672, 387, 800, 928, 768, 352, 368, 608, 930,
             624, 896, 1072, 1168, 656, 931, 688, 816, 899, 944, 945, 784, 1056, 897,
-            898, 946, 1024, 914, 913, 916, 1200, 915, 947, 1152, 918, 912, 929, 1184,
-            919, 917,
+            898, 946, 1024, 914, 913, 916, 1200, 915, 947, 1152, 926, 920, 929, 1184,
+            927, 925,
         ),
         (
             16, 160, 0, 50, 1, 49, 51, 161, 2, 3, 1313, 48, 128, 17,
@@ -114,15 +114,15 @@
             386, 528, 1296, 1329, 1297, 385, 1328, 640, 288, 304, 402, 320, 560, 336,
             403, 768, 896, 419, 576, 544, 897, 352, 368, 899, 898, 608, 592, 656,
             624, 1040, 784, 688, 1072, 912, 672, 1024, 1056, 913, 816, 1168, 914, 944,
-            945, 915, 800, 946, 1152, 930, 1184, 928, 931, 1200, 947, 932, 934, 933,
-            929, 935,
+            945, 915, 800, 946, 1152, 930, 1184, 928, 931, 1200, 947, 940, 942, 933,
+            937, 943,
         ),
         (
             16, 0, 176, 32, 2, 1328, 1, 177, 3, 128, 129, 1280, 17, 1281,
             1329, 256, 18, 272, 386, 512, 19, 528, 144, 33, 34, 145, 640, 35,
             1296, 160, 768, 1297, 161, 385, 288, 304, 1312, 544, 402, 560, 1313, 1040,
             656, 320, 784, 336, 387, 1024, 592, 576, 1056, 419, 403, 352, 672, 368,
-            1168, 800, 624, 608, 1072, 1184, 688, 1152, 816, 1200, 944, 946, 945, 947,
+            1168, 800, 624, 608, 1072, 1184, 688, 1152, 816, 1200, 952, 954, 953, 955,
         ),
     ),
 }
@@ -161,8 +161,8 @@
 
 
 def fused_kernel(
-    lines, rows, count, packed, strip, history, coupling, dyson, later_out, wide,
-    later, hist, weight, blocks, parts, first, keep, sums, joined, own, new, tau, source, near, taus,
+    lines, rows, count, packed, strip, history, coupling, inverse, later_out, wide,
+    dyson, later, hist, weight, blocks, parts, first, keep, sums, joined, own, new, tau, source, near, taus,
     give, take, stage, land, held,
     hop_s, hop_r, pair_s, pair_r, sum_s, sum_r, tau_s, tau_r, near_s, near_r, local,
     give_s, give_r, chain_s, chain_r,
@@ -203,36 +203,39 @@
     def hop(way, m, k):
         block = blocks.at[2 * m + core, :, cut(k)]
         to = 2 * (q + 1 - 2 * way) + core
-        return remote(block, block, hop_s.at[way, m, k], hop_r.at[m, k], row, to)
+        return remote(block, block, hop_s.at[way, m], hop_r.at[m, k], row, to)
+
+    def settle(ref, send_sem, recv_sem):
+        return remote(ref, ref, send_sem, recv_sem, row, 2 * q + 1 - core)
 
     def pair(m, k):
         block = blocks.at[2 * m + core, :, cut(k)]
-        return remote(block, block, pair_s.at[m, k], pair_r.at[m, k], row, 2 * q + 1 - core)
+        return remote(block, block, pair_s.at[0], pair_r.at[m], row, 2 * q + 1 - core)
 
     def send_parts(j, k):
         return remote(
-            parts.at[j, k], first.at[j, k], sum_s.at[j, k], sum_r.at[j, k], direct[k], col
+            parts.at[j, k], first.at[j, k], sum_s.at[k], sum_r.at[j, k], direct[k], col
         )
 
     def send_joined(j, k):
         return remote(
-            sums.at[j, k], joined.at[j, k], sum_s.at[j, 2 + k], sum_r.at[j, 2 + k],
+            sums.at[j, k], joined.at[j, k], sum_s.at[2 + k], sum_r.at[j, 2 + k],
             direct[1 - k], col,
         )
 
     def send_tau(j, k):
         block = taus.at[row, :, span(j)]
-        return remote(block, block, tau_s.at[j, k], tau_r.at[j, k], direct[k], col)
+        return remote(block, block, tau_s.at[k], tau_r.at[j, k], direct[k], col)
 
     def relay_tau(j, k):
         block = taus.at[direct[k], k, span(j)]
-        return remote(block, block, tau_s.at[j, 2 + k], tau_r.at[j, 2 + k], direct[1 - k], col)
+        return remote(block, block, tau_s.at[2 + k], tau_r.at[j, 2 + k], direct[1 - k], col)
 
     def send_near(m, k):
         return remote(
             near.at[:, double(m)],
             wide.at[:, double(m), columns(row)],
-            near_s.at[m, k],
+            near_s.at[k],
             near_r.at[m, k],
             direct[k],
             col,
@@ -240,7 +243,7 @@
 
     def relay_near(m, k):
         block = wide.at[k, double(m), columns(direct[k])]
-        return remote(block, block, near_s.at[m, 2 + k], near_r.at[m, 2 + k], direct[1 - k], col)
+        return remote(block, block, near_s.at[2 + k], near_r.at[m, 2 + k], direct[1 - k], col)
 
     def own_near(m):
         return pltpu.make_async_copy(
@@ -248,7 +251,7 @@
         )
 
     def swap(d):
-        return remote(give.at[d], take.at[d], give_s.at[d], give_r.at[d], row, 2 * q + 1 - core)
+        return remote(give.at[d], take.at[d], give_s.at[0], give_r.at[d], row, 2 * q + 1 - core)
 
     def chain(way, d, k):
         to = q + 1 - 2 * way
@@ -256,7 +259,7 @@
         return remote(
             stage.at[d, :, cut(k)],
             land.at[slot, :, cut(k)],
-            chain_s.at[d, k],
+            chain_s.at[0],
             chain_r.at[slot, k],
             row,
             2 * to + core,
@@ -315,8 +318,8 @@
     def op_product(m, other):
         @pl.when(other == 1)
         def _():
-            for k in range(CHUNKS):
-                pair(m, k).wait_recv()
+            block = blocks.at[2 * m + 1 - core]
+            settle(block, pair_s.at[0], pair_r.at[m]).wait_recv()
 
         j = 2 * m + core + other - 2 * core * other
         real = mm(blocks[j, 0], hist[0], NN) - mm(blocks[j, 1], hist[1], NN)
@@ -445,13 +448,13 @@
                     held[held_at(d), p] = pair_sums[p] + take[d, p].astype(jnp.float32)
 
     def op_chain(d, b):
-        way, k = lax.div(b, CHUNKS), lax.rem(b, CHUNKS)
+        ends, way, k = lax.div(b, 2 * CHUNKS), lax.rem(lax.div(b, CHUNKS), 2), lax.rem(b, CHUNKS)
         at = cut(k)
         slot = jnp.where(way == 1, lines, d)
         pltpu.make_async_remote_copy(
             src_ref=stage.at[d, :, at],
             dst_ref=land.at[slot, :, at],
-            send_sem=chain_s.at[d, k],
+            send_sem=chain_s.at[0],
             recv_sem=chain_r.at[slot, k],
             device_id=(row, 2 * q + 1 - core),
             device_id_type=MESH,
@@ -462,6 +465,12 @@
             for p in (0, 1):
                 later[p, at, :] += land[slot, p, at, :].astype(jnp.float32)
 
+            @pl.when(ends == 1)
+            def _():
+                pltpu.make_async_copy(
+                    later.at[:, at], later_out.at[:, at], local.at[lines]
+                ).start()
+
         @pl.when(d != q)
         def _():
             for p in (0, 1):
@@ -482,8 +491,10 @@
 
     load_hist = pltpu.make_async_copy(history, hist, local.at[lines])
     load_strip = pltpu.make_async_copy(strip, later, local.at[lines + 1])
+    load_dyson = pltpu.make_async_copy(inverse, dyson, local.at[lines + 2])
     load_strip.start()
     load_hist.start()
+    load_dyson.start()
     entry_barrier(row, q, core, lines, rows, False)
     place_row = lax.broadcasted_iota(jnp.int32, (orbitals, share), 0)
     place_col = lax.rem(lax.broadcasted_iota(jnp.int32, (orbitals, share), 1), orbitals)
@@ -530,6 +541,7 @@
 
     lax.fori_loop(0, total, clear, 0)
     load_hist.wait()
+    load_dyson.wait()
 
     words = []
     for w in range(count // 2):
@@ -589,45 +601,35 @@
         return c
 
     lax.fori_loop(0, count, step, 0)
-    leave = pltpu.make_async_copy(later, later_out, local.at[lines])
-    leave.start()
-
-    def drain_line(m, c):
-        for k in range(CHUNKS):
-
-            @pl.when(jnp.logical_and(m <= q, q < last))
-            def _():
-                hop(0, m, k).wait_send()
-
-            @pl.when(jnp.logical_and(m >= q, q > 0))
-            def _():
-                hop(1, m, k).wait_send()
-
-            pair(m, k).wait_send()
-
-            @pl.when(m != q)
-            def _():
-                chain(0, m, k).wait_send()
-
-        swap(m).wait_send()
+
+    def drain(m, c):
+        block = blocks.at[2 * m + core]
+
+        @pl.when(jnp.logical_and(m <= q, q < last))
+        def _():
+            settle(block, hop_s.at[0, m], hop_r.at[m, 0]).wait_send()
+
+        @pl.when(jnp.logical_and(m >= q, q > 0))
+        def _():
+            settle(block, hop_s.at[1, m], hop_r.at[m, 0]).wait_send()
+
         own_near(m).wait()
         for k in (0, 1):
-            send_near(m, k).wait_send()
-            relay_near(m, k).wait()
+            relay_near(m, k).wait_recv()
         return c
 
-    lax.fori_loop(0, lines, drain_line, 0)
-
-    def drain_block(j, c):
-        for k in (0, 1):
-            send_parts(j, k).wait_send()
-            send_joined(j, k).wait_send()
-            send_tau(j, k).wait_send()
-            relay_tau(j, k).wait_send()
-        return c
-
-    lax.fori_loop(0, 2 * lines, drain_block, 0)
-    leave.wait()
+    lax.fori_loop(0, lines, drain, 0)
+    settle(blocks.at[pl.ds(0, lines)], pair_s.at[0], pair_r.at[0]).wait_send()
+    for k in (0, 1):
+        settle(parts.at[:, k], sum_s.at[k], sum_r.at[0, 0]).wait_send()
+        settle(sums.at[:, k], sum_s.at[2 + k], sum_r.at[0, 0]).wait_send()
+        settle(taus.at[k], tau_s.at[k], tau_r.at[0, 0]).wait_send()
+        settle(taus.at[0, k], tau_s.at[2 + k], tau_r.at[0, 0]).wait_send()
+        settle(near, near_s.at[k], near_r.at[0, 0]).wait_send()
+        settle(near.at[k], near_s.at[2 + k], near_r.at[0, 0]).wait_send()
+    settle(give, give_s.at[0], give_r.at[0]).wait_send()
+    settle(stage.at[pl.ds(0, last)], chain_s.at[0], chain_r.at[0, 0]).wait_send()
+    pltpu.make_async_copy(later, later_out, local.at[lines]).wait()
 
 
 VMEM = pl.BlockSpec(memory_space=pltpu.VMEM)
@@ -650,9 +652,10 @@
             jax.ShapeDtypeStruct(strip.shape, f32),
             jax.ShapeDtypeStruct((2, full, width), bf16),
         ),
-        in_specs=[ANY, ANY, SMEM, SMEM],
+        in_specs=[ANY, ANY, SMEM, ANY],
         out_specs=(ANY, ANY),
         scratch_shapes=[
+            pltpu.SMEM(dyson.shape, f32),
             pltpu.VMEM(strip.shape, f32),
             pltpu.VMEM(history.shape, bf16),
             pltpu.VMEM((coupling.shape[0], share), f32),
@@ -673,20 +676,20 @@
             pltpu.VMEM((lines, 2, height, depth), bf16),
             pltpu.VMEM((lines + 1, 2, height, depth), bf16),
             pltpu.VMEM((lines - 1, 2, height, depth), f32),
-            DMA((2, lines, CHUNKS)),
+            DMA((2, lines)),
             DMA((lines, CHUNKS)),
-            DMA((lines, CHUNKS)),
-            DMA((lines, CHUNKS)),
+            DMA((1,)),
+            DMA((lines,)),
+            DMA((4,)),
             DMA((blocks, 4)),
+            DMA((4,)),
             DMA((blocks, 4)),
-            DMA((blocks, 4)),
-            DMA((blocks, 4)),
+            DMA((4,)),
             DMA((lines, 4)),
-            DMA((lines, 4)),
-            DMA((lines + 2,)),
+            DMA((lines + 3,)),
+            DMA((1,)),
             DMA((lines,)),
-            DMA((lines,)),
-            DMA((lines, CHUNKS)),
+            DMA((1,)),
             DMA((lines + 1, CHUNKS)),
         ],
         compiler_params=pltpu.CompilerParams(

time: 161 us -> 157 us (0.975)
  Pallas kernels: 160 us -> 156 us
    pallas_call x1, Pallas kernels: 154 us -> 150 us  [fused(): pl.pallas_call(functools.partial(fused_kernel, lines, rows, count, packed...]
where the time goes in v3:
time: 157 us
  Pallas kernels  156 us (99%)
    pallas_call x1, Pallas kernels, fused(): pl.pallas_call(functools.partial(fused_kernel, lines, rows, count, packed...  150 us
    pallas_call x1, Pallas kernels, widen(): pl.pallas_call(functools.partial(widen_kernel, pieces), out_shape=(jax.Sh...  6.18 us

profile of v3, /device:TPU:27, one launch (start us, length us, event | category | flops | bytes accessed | tf_op | source)
XLA Modules:
  0.0 156.5 jit_solution(1589647101506749207)
XLA Ops:
  0.6 149.7 %group_updates.1 = (f32[2,256,1024]{2,1,0:T(8,128)}, bf16[2,2048,512]{2,1,0:T(8,128)(2,1)}) custom-call(f32[2,256,1024]{2,1,0:T(8,128)} %strip.1, bf16[2,1024,512]{2,1,0:T(8,128)(2,1)} %history.1, f32[32]{0:T(128)} %coupling.1, f32[2,2,64,64]{3,2,1,0:T(8,128)} %inverse.1), custom_call_target="tpu_custom_call" | custom-call | tf_op jit(solution)/shard_map/group_updates/pallas_call | solution.py:649
  150.4 6.2 %widen.1 = (f32[2,2048,512]{2,1,0:T(8,128)}, f32[2,256,1024]{2,1,0:T(8,128)}) custom-call(bf16[2,2048,512]{2,1,0:T(8,128)(2,1)} %get-tuple-element.4.wide, f32[2,256,1024]{2,1,0:T(8,128)} %get-tuple-element.5.later), custom_call_target="tpu_custom_call" | custom-call | tf_op jit(solution)/shard_map/widen/pallas_call | solution.py:730

commit v4 on v3

--- a/solution.py
+++ b/solution.py
@@ -57,22 +57,21 @@
 MESH = pl.DeviceIdType.MESH
 NN = (((1,), (0,)), ((), ()))
 NT = (((1,), (1,)), ((), ()))
-CHUNKS = 4
+CHUNKS = 8
 HEAD = 4
-(
-    RELAY,
-    PRODUCT,
-    SOLVE,
-    UPDATE,
-    SPREAD_TAU,
-    GIVE,
-    KEEP,
-    CHAIN,
-    SEND_NEAR,
-    RELAY_NEAR,
-    JOIN,
-    NOTHING,
-) = range(12)
+LINKS = 4
+RELAY, UPDATE, PRODUCT, JOIN, SOLVE, SPREAD_TAU, SECOND, SEND_NEAR, RELAY_NEAR, NOTHING = (
+    64,
+    96,
+    112,
+    128,
+    144,
+    152,
+    160,
+    168,
+    172,
+    176,
+)
 
 
 def mm(x, y, dims):
@@ -93,47 +92,53 @@
 ORDERS = {
     4: (
         (
-            128, 129, 1280, 1281, 256, 272, 18, 1024, 17, 386, 16, 19, 144, 145,
-            385, 1296, 32, 1297, 288, 304, 544, 35, 402, 560, 34, 33, 161, 656,
-            160, 784, 1313, 1312, 51, 403, 320, 336, 50, 387, 576, 48, 49, 592,
-            176, 177, 672, 1328, 800, 1329, 419, 528, 352, 368, 608, 624, 1072, 1056,
-            688, 1152, 816, 1040, 512, 640, 1168, 768, 908, 909, 1184, 911, 1200, 910,
+            113, 112, 114, 115, 128, 129, 130, 131, 144, 145, 72, 97, 152, 118, 116, 153,
+            134, 73, 117, 119, 133, 132, 135, 168, 99, 146, 147, 80, 98, 120, 154, 102,
+            155, 122, 136, 81, 121, 123, 161, 138, 165, 137, 139, 103, 148, 149, 88, 156,
+            126, 157, 89, 125, 127, 162, 124, 166, 141, 143, 142, 140, 107, 150, 151, 158,
+            160, 159, 170, 172, 163, 171, 167, 169, 174, 164, 175, 173, 14, 12, 15, 13,
         ),
         (
-            0, 145, 144, 32, 1, 2, 34, 35, 1296, 3, 33, 129, 128, 1280,
-            160, 1281, 1297, 50, 161, 256, 51, 272, 385, 288, 48, 1313, 304, 1312,
-            49, 177, 512, 402, 386, 528, 176, 320, 336, 576, 1329, 544, 419, 592,
-            640, 1040, 1328, 403, 560, 672, 387, 800, 928, 768, 352, 368, 608, 930,
-            624, 896, 1072, 1168, 656, 931, 688, 816, 899, 944, 945, 784, 1056, 897,
-            898, 946, 1024, 914, 913, 916, 1200, 915, 947, 1152, 926, 920, 929, 1184,
-            927, 925,
+            116, 119, 64, 117, 65, 118, 132, 66, 67, 135, 133, 134, 112, 114, 68, 80,
+            122, 69, 128, 130, 70, 120, 71, 113, 115, 81, 121, 129, 131, 136, 138, 137,
+            123, 144, 145, 88, 97, 139, 124, 126, 146, 152, 153, 98, 147, 103, 154, 142,
+            89, 125, 127, 140, 155, 102, 148, 149, 99, 161, 156, 141, 143, 107, 157, 150,
+            151, 162, 165, 16, 158, 159, 17, 166, 170, 32, 160, 164, 169, 1, 163, 19,
+            34, 3, 174, 167, 168, 35, 2, 18, 48, 171, 172, 49, 0, 173, 175, 28,
+            50, 30, 51, 29, 33, 31,
         ),
         (
-            16, 160, 0, 50, 1, 49, 51, 161, 2, 3, 1313, 48, 128, 17,
-            129, 176, 1312, 18, 1281, 1280, 177, 19, 256, 145, 144, 272, 512, 387,
-            386, 528, 1296, 1329, 1297, 385, 1328, 640, 288, 304, 402, 320, 560, 336,
-            403, 768, 896, 419, 576, 544, 897, 352, 368, 899, 898, 608, 592, 656,
-            624, 1040, 784, 688, 1072, 912, 672, 1024, 1056, 913, 816, 1168, 914, 944,
-            945, 915, 800, 946, 1152, 930, 1184, 928, 931, 1200, 947, 940, 942, 933,
-            937, 943,
+            120, 122, 121, 138, 123, 136, 137, 64, 65, 139, 66, 67, 112, 88, 124, 68,
+            128, 89, 69, 140, 114, 127, 70, 130, 71, 113, 73, 72, 115, 143, 126, 129,
+            75, 74, 116, 131, 142, 132, 77, 118, 144, 78, 76, 79, 117, 119, 145, 134,
+            97, 135, 133, 152, 98, 153, 146, 147, 99, 154, 102, 155, 125, 148, 160, 103,
+            141, 164, 1, 156, 149, 0, 107, 150, 157, 161, 3, 158, 151, 165, 2, 162,
+            159, 171, 16, 169, 163, 166, 168, 32, 170, 17, 167, 173, 18, 19, 48, 35,
+            172, 49, 175, 50, 51, 34, 37, 46, 174, 47, 44, 41,
         ),
         (
-            16, 0, 176, 32, 2, 1328, 1, 177, 3, 128, 129, 1280, 17, 1281,
-            1329, 256, 18, 272, 386, 512, 19, 528, 144, 33, 34, 145, 640, 35,
-            1296, 160, 768, 1297, 161, 385, 288, 304, 1312, 544, 402, 560, 1313, 1040,
-            656, 320, 784, 336, 387, 1024, 592, 576, 1056, 419, 403, 352, 672, 368,
-            1168, 800, 624, 608, 1072, 1184, 688, 1152, 816, 1200, 952, 954, 953, 955,
+            125, 126, 124, 141, 127, 140, 81, 83, 80, 82, 120, 143, 122, 142, 136, 66,
+            65, 64, 67, 138, 112, 128, 68, 69, 114, 70, 71, 113, 115, 129, 131, 130,
+            144, 145, 97, 74, 152, 73, 77, 72, 153, 75, 118, 116, 76, 78, 160, 79,
+            117, 119, 134, 164, 133, 84, 132, 85, 86, 135, 87, 121, 123, 146, 147, 102,
+            139, 154, 155, 137, 168, 98, 161, 148, 165, 149, 172, 107, 156, 103, 157, 99,
+            150, 151, 162, 171, 166, 158, 159, 175, 169, 170, 163, 167, 56, 173, 58, 174,
+            57, 59,
         ),
     ),
 }
 
 def step_words(lines):
     longest = max(len(steps) for steps in ORDERS[lines])
-    longest += longest % 2
+    longest += -longest % 4
     packed = []
     for steps in ORDERS[lines]:
-        codes = list(steps) + [NOTHING * 128] * (longest - len(steps))
-        packed.append([codes[i] + 2048 * codes[i + 1] for i in range(0, longest, 2)])
+        codes = list(steps) + [NOTHING] * (longest - len(steps))
+        words = []
+        for i in range(0, longest, 4):
+            word = sum(code << (8 * k) for k, code in enumerate(codes[i : i + 4]))
+            words.append(word - (1 << 32) * (word >> 31))
+        packed.append(words)
     return longest, packed
 
 
@@ -177,6 +182,8 @@
     times = height // orbitals
     total = times * 2 * lines
     piece = height // CHUNKS
+    length = height // LINKS
+    half = height // 2
     beside = row + 1 - 2 * lax.rem(row, 2)
     across = lax.rem(row + 2, 4)
     direct = [beside, across]
@@ -194,6 +201,12 @@
     def cut(k):
         return pl.ds(pl.multiple_of(k * piece, piece), piece)
 
+    def link(k):
+        return pl.ds(pl.multiple_of(k * length, length), length)
+
+    def side(h):
+        return pl.ds(pl.multiple_of(h * half, half), half)
+
     def columns(r):
         return pl.ds(pl.multiple_of(r * share, share), share)
 
@@ -210,17 +223,27 @@
 
     def pair(m, k):
         block = blocks.at[2 * m + core, :, cut(k)]
-        return remote(block, block, pair_s.at[0], pair_r.at[m], row, 2 * q + 1 - core)
-
-    def send_parts(j, k):
+        there = pair_r.at[m, k // (CHUNKS // 2)]
+        return remote(block, block, pair_s.at[0], there, row, 2 * q + 1 - core)
+
+    def send_parts(j, h, k):
         return remote(
-            parts.at[j, k], first.at[j, k], sum_s.at[k], sum_r.at[j, k], direct[k], col
+            parts.at[j, k, :, side(h)],
+            first.at[j, k, :, side(h)],
+            sum_s.at[k],
+            sum_r.at[j, h, k],
+            direct[k],
+            col,
         )
 
-    def send_joined(j, k):
+    def send_joined(j, h, k):
         return remote(
-            sums.at[j, k], joined.at[j, k], sum_s.at[2 + k], sum_r.at[j, 2 + k],
-            direct[1 - k], col,
+            sums.at[j, k, side(h)],
+            joined.at[j, k, side(h)],
+            sum_s.at[2 + k],
+            sum_r.at[j, h, 2 + k],
+            direct[1 - k],
+            col,
         )
 
     def send_tau(j, k):
@@ -257,8 +280,8 @@
         to = q + 1 - 2 * way
         slot = jnp.where(jnp.logical_and(d == to, way == 1), lines, d)
         return remote(
-            stage.at[d, :, cut(k)],
-            land.at[slot, :, cut(k)],
+            stage.at[d, :, link(k)],
+            land.at[slot, :, link(k)],
             chain_s.at[0],
             chain_r.at[slot, k],
             row,
@@ -276,37 +299,51 @@
 
     def update(acc, src, group, low, n, j):
         def add(i, c):
-            at = low + i
-            real, imag = acc[0, slab(at), :], acc[1, slab(at), :]
+            lines_at = [low + 2 * i, low + 2 * i + 1]
+            sums3 = []
+            for at in lines_at:
+                real, imag = acc[0, slab(at), :], acc[1, slab(at), :]
+                sums3.append([real, jnp.zeros_like(real), real + imag])
             for t in range(times):
                 m = j * times + t
-                dr, di = dyson[group, 0, at, m], dyson[group, 1, at, m]
-                sr = src[0, slab(m), :].astype(jnp.float32)
-                si = src[1, slab(m), :].astype(jnp.float32)
-                real += dr * sr - di * si
-                imag += dr * si + di * sr
-            acc[0, slab(at), :] = real
-            acc[1, slab(at), :] = imag
+                planes = [src[p, slab(m), :] for p in (0, 1, 2)]
+                for at, three in zip(lines_at, sums3):
+                    dr, di = dyson[group, 0, at, m], dyson[group, 1, at, m]
+                    for p, d in enumerate((dr, di, dr + di)):
+                        three[p] = three[p] + d * planes[p]
+            for at, three in zip(lines_at, sums3):
+                acc[0, slab(at), :] = three[0] - three[1]
+                acc[1, slab(at), :] = three[2] - three[0] - three[1]
             return c
 
-        lax.fori_loop(0, n, add, 0)
-
-    def op_relay(m, k):
-        hop(0, m, k).wait_recv()
-
-        @pl.when(jnp.logical_and(m < q, q < last))
-        def _():
-            hop(0, m, k).start()
-
-        @pl.when(jnp.logical_and(m > q, q > 0))
-        def _():
-            hop(1, m, k).start()
-
-        pair(m, k).start()
-
-        @pl.when(jnp.logical_and(m == q - 1, k == CHUNKS - 1))
-        def _():
-            rest()
+        lax.fori_loop(0, n // 2, add, 0)
+
+    def op_relay(m, b):
+        @pl.when(m < q)
+        def _():
+            hop(0, m, b).wait_recv()
+
+            @pl.when(q < last)
+            def _():
+                hop(0, m, b).start()
+
+            pair(m, b).start()
+
+            @pl.when(jnp.logical_and(m == q - 1, b == CHUNKS - 1))
+            def _():
+                rest()
+
+        @pl.when(m > q)
+        def _():
+            for x in range(CHUNKS // 2):
+                k = b * (CHUNKS // 2) + x
+                hop(1, m, k).wait_recv()
+
+                @pl.when(q > 0)
+                def _():
+                    hop(1, m, k).start()
+
+                pair(m, k).start()
 
     def rest():
         for x in range(CHUNKS):
@@ -315,15 +352,20 @@
             def _():
                 hop(0, q, x).start()
 
-    def op_product(m, other):
+    def op_product(m, b):
+        other, h = lax.div(b, 2), lax.rem(b, 2)
+        at = side(h)
+
         @pl.when(other == 1)
         def _():
-            block = blocks.at[2 * m + 1 - core]
-            settle(block, pair_s.at[0], pair_r.at[m]).wait_recv()
+            block = blocks.at[2 * m + 1 - core, :, at]
+            settle(block, pair_s.at[0], pair_r.at[m, h]).wait_recv()
 
         j = 2 * m + core + other - 2 * core * other
-        real = mm(blocks[j, 0], hist[0], NN) - mm(blocks[j, 1], hist[1], NN)
-        imag = mm(blocks[j, 0], hist[1], NN) + mm(blocks[j, 1], hist[0], NN)
+        real_in, imag_in = blocks[j, 0, at, :], blocks[j, 1, at, :]
+        real = mm(real_in, hist[0], NN) - mm(imag_in, hist[1], NN)
+        imag = mm(real_in, hist[1], NN) + mm(imag_in, hist[0], NN)
+        own_at = pl.ds(pl.multiple_of(j * height + h * half, half), half)
         for r in range(rows):
 
             @pl.when(row == r)
@@ -331,32 +373,37 @@
                 mine, near_x, near_y, far = [
                     slice(x * share, (x + 1) * share) for x in (r, r ^ 1, r ^ 2, r ^ 3)
                 ]
-                parts[j, 0, 0] = real[:, near_x].astype(bf16)
-                parts[j, 0, 1] = real[:, far].astype(bf16)
-                parts[j, 1, 0] = imag[:, near_y].astype(bf16)
-                parts[j, 1, 1] = imag[:, far].astype(bf16)
-                keep[j, 0] = real[:, near_y]
-                keep[j, 1] = imag[:, near_x]
-                own[0, span(j), :] = real[:, mine]
-                own[1, span(j), :] = imag[:, mine]
-
-        for k in (0, 1):
-            send_parts(j, k).start()
-
-    def op_join(m, other):
+                parts[j, 0, 0, at, :] = real[:, near_x].astype(bf16)
+                parts[j, 0, 1, at, :] = real[:, far].astype(bf16)
+                parts[j, 1, 0, at, :] = imag[:, near_y].astype(bf16)
+                parts[j, 1, 1, at, :] = imag[:, far].astype(bf16)
+                keep[j, 0, at, :] = real[:, near_y]
+                keep[j, 1, at, :] = imag[:, near_x]
+                own[0, own_at, :] = real[:, mine]
+                own[1, own_at, :] = imag[:, mine]
+
+        for k in (0, 1):
+            send_parts(j, h, k).start()
+
+    def op_join(m, b):
+        other, h = lax.div(b, 2), lax.rem(b, 2)
+        at = side(h)
         j = 2 * m + core + other - 2 * core * other
         for k in (0, 1):
-            send_parts(j, k).wait_recv()
-            sums[j, k] = (keep[j, k] + first[j, k, 1].astype(jnp.float32)).astype(bf16)
-        for k in (0, 1):
-            send_joined(j, k).start()
+            send_parts(j, h, k).wait_recv()
+            value = keep[j, k, at, :] + first[j, k, 1, at, :].astype(jnp.float32)
+            sums[j, k, at, :] = value.astype(bf16)
+        for k in (0, 1):
+            send_joined(j, h, k).start()
 
     def op_solve(j):
         at = span(j)
         for p in (0, 1):
-            send_joined(j, p).wait_recv()
+            for h in (0, 1):
+                send_joined(j, h, p).wait_recv()
             others = first[j, p, 0].astype(jnp.float32) + joined[j, p].astype(jnp.float32)
             own[p, at, :] = TIME_STEP * (own[p, at, :] + others)
+        own[2, at, :] = own[0, at, :] + own[1, at, :]
 
         @pl.when(lax.rem(j, 2) == 1)
         def _():
@@ -370,8 +417,11 @@
             near[0, rows_at, :] = real.astype(bf16)
             near[1, rows_at, :] = imag.astype(bf16)
             factor = weight[...] * (real * real + imag * imag)
-            source[0, rows_at, :] = (real * factor).astype(bf16)
-            source[1, rows_at, :] = (imag * factor).astype(bf16)
+            sigma_real = (real * factor).astype(bf16).astype(jnp.float32)
+            sigma_imag = (imag * factor).astype(bf16).astype(jnp.float32)
+            source[0, rows_at, :] = sigma_real
+            source[1, rows_at, :] = sigma_imag
+            source[2, rows_at, :] = sigma_real + sigma_imag
             return c
 
         lax.fori_loop(0, times, sigma, 0)
@@ -439,7 +489,7 @@
                 for p in (0, 1):
                     value = pair_sums[p] + take[d, p].astype(jnp.float32)
                     stage[d, p] = value.astype(bf16)
-                for k in range(CHUNKS):
+                for k in range(LINKS):
                     chain_on(d, k)
 
             @pl.when(jnp.logical_and(d != q, jnp.logical_not(begins)))
@@ -448,8 +498,8 @@
                     held[held_at(d), p] = pair_sums[p] + take[d, p].astype(jnp.float32)
 
     def op_chain(d, b):
-        ends, way, k = lax.div(b, 2 * CHUNKS), lax.rem(lax.div(b, CHUNKS), 2), lax.rem(b, CHUNKS)
-        at = cut(k)
+        ends, way, k = lax.div(b, 2 * LINKS), lax.rem(lax.div(b, LINKS), 2), lax.rem(b, LINKS)
+        at = link(k)
         slot = jnp.where(way == 1, lines, d)
         pltpu.make_async_remote_copy(
             src_ref=stage.at[d, :, at],
@@ -544,59 +594,72 @@
     load_dyson.wait()
 
     words = []
-    for w in range(count // 2):
+    for w in range(count // 4):
         word = jnp.int32(packed[last][w])
         for x in range(last):
             word = jnp.where(q == x, jnp.int32(packed[x][w]), word)
         words.append(word)
 
     def step(i, c):
-        which, place = lax.div(i, 2), lax.rem(i, 2)
-        word = words[0]
-        for w in range(1, len(words)):
-            word = jnp.where(which == w, words[w], word)
-        code = jnp.where(place == 1, lax.div(word, 2048), lax.rem(word, 2048))
-        kind, a, b = lax.div(code, 128), lax.rem(lax.div(code, 16), 8), lax.rem(code, 16)
-
-        @pl.when(kind == RELAY)
-        def _():
-            op_relay(a, b)
-
-        @pl.when(kind == PRODUCT)
-        def _():
-            op_product(a, b)
-
-        @pl.when(kind == JOIN)
-        def _():
-            op_join(a, b)
-
-        @pl.when(kind == SOLVE)
-        def _():
-            op_solve(a)
-
-        @pl.when(kind == UPDATE)
-        def _():
-            op_update(a, b)
-
-        @pl.when(kind == SPREAD_TAU)
-        def _():
-            op_spread_tau(a)
-
-        @pl.when(jnp.logical_or(kind == GIVE, kind == KEEP))
-        def _():
-            op_second(a, kind - GIVE)
-
-        @pl.when(kind == CHAIN)
-        def _():
-            op_chain(a, b)
-
-        @pl.when(kind == SEND_NEAR)
-        def _():
-            op_send_near(a)
-
-        @pl.when(kind == RELAY_NEAR)
-        def _():
-            op_relay_near(a)
+        which, place = lax.div(i, 4), lax.rem(i, 4)
+        level = words
+        bit = 1
+        while len(level) > 1:
+            odd = lax.rem(lax.div(which, bit), 2) == 1
+            joined_up = [
+                jnp.where(odd, level[w + 1], level[w]) for w in range(0, len(level) - 1, 2)
+            ]
+            level = joined_up + level[len(level) - len(level) % 2 :]
+            bit *= 2
+        code = lax.shift_right_logical(level[0], 8 * place) & 255
+
+        @pl.when(code < UPDATE)
+        def _():
+            @pl.when(code < RELAY)
+            def _():
+                op_chain(lax.div(code, 16), lax.rem(code, 16))
+
+            @pl.when(code >= RELAY)
+            def _():
+                op_relay(lax.div(code - RELAY, 8), lax.rem(code, 8))
+
+        @pl.when(jnp.logical_and(code >= UPDATE, code < SOLVE))
+        def _():
+            a, b = lax.rem(lax.div(code, 4), 4), lax.rem(code, 4)
+
+            @pl.when(code < PRODUCT)
+            def _():
+                op_update(a, b)
+
+            @pl.when(jnp.logical_and(code >= PRODUCT, code < JOIN))
+            def _():
+                op_product(a, b)
+
+            @pl.when(code >= JOIN)
+            def _():
+                op_join(a, b)
+
+        @pl.when(code >= SOLVE)
+        def _():
+            @pl.when(code < SPREAD_TAU)
+            def _():
+                op_solve(code - SOLVE)
+
+            @pl.when(jnp.logical_and(code >= SPREAD_TAU, code < SECOND))
+            def _():
+                op_spread_tau(code - SPREAD_TAU)
+
+            @pl.when(jnp.logical_and(code >= SECOND, code < SEND_NEAR))
+            def _():
+                op_second(lax.rem(code, 4), lax.div(code - SECOND, 4))
+
+            @pl.when(jnp.logical_and(code >= SEND_NEAR, code < RELAY_NEAR))
+            def _():
+                op_send_near(code - SEND_NEAR)
+
+            @pl.when(jnp.logical_and(code >= RELAY_NEAR, code < NOTHING))
+            def _():
+                op_relay_near(code - RELAY_NEAR)
 
         return c
 
@@ -619,10 +682,10 @@
         return c
 
     lax.fori_loop(0, lines, drain, 0)
-    settle(blocks.at[pl.ds(0, lines)], pair_s.at[0], pair_r.at[0]).wait_send()
+    settle(blocks.at[pl.ds(0, lines)], pair_s.at[0], pair_r.at[0, 0]).wait_send()
     for k in (0, 1):
-        settle(parts.at[:, k], sum_s.at[k], sum_r.at[0, 0]).wait_send()
-        settle(sums.at[:, k], sum_s.at[2 + k], sum_r.at[0, 0]).wait_send()
+        settle(parts.at[:, k], sum_s.at[k], sum_r.at[0, 0, 0]).wait_send()
+        settle(sums.at[:, k], sum_s.at[2 + k], sum_r.at[0, 0, 0]).wait_send()
         settle(taus.at[k], tau_s.at[k], tau_r.at[0, 0]).wait_send()
         settle(taus.at[0, k], tau_s.at[2 + k], tau_r.at[0, 0]).wait_send()
         settle(near, near_s.at[k], near_r.at[0, 0]).wait_send()
@@ -665,10 +728,10 @@
             pltpu.VMEM((blocks, 2, height, share), f32),
             pltpu.VMEM((blocks, 2, height, share), bf16),
             pltpu.VMEM((blocks, 2, height, share), bf16),
+            pltpu.VMEM((3, full, share), f32),
             pltpu.VMEM((2, full, share), f32),
             pltpu.VMEM((2, full, share), f32),
-            pltpu.VMEM((2, full, share), f32),
-            pltpu.VMEM((2, full, share), bf16),
+            pltpu.VMEM((3, full, share), f32),
             pltpu.VMEM((2, full, share), bf16),
             pltpu.VMEM((rows, 2, full, share), bf16),
             pltpu.VMEM((lines, 2, height, depth), bf16),
@@ -679,9 +742,9 @@
             DMA((2, lines)),
             DMA((lines, CHUNKS)),
             DMA((1,)),
-            DMA((lines,)),
+            DMA((lines, 2)),
             DMA((4,)),
-            DMA((blocks, 4)),
+            DMA((blocks, 2, 4)),
             DMA((4,)),
             DMA((blocks, 4)),
             DMA((4,)),
@@ -690,7 +753,7 @@
             DMA((1,)),
             DMA((lines,)),
             DMA((1,)),
-            DMA((lines + 1, CHUNKS)),
+            DMA((lines + 1, LINKS)),
         ],
         compiler_params=pltpu.CompilerParams(
             collective_id=0, has_side_effects=True, vmem_limit_bytes=63 * 1024 * 1024
@@ -782,6 +845,8 @@
         and share_cols == 128
         and share_cols % orbitals == 0
         and strip_rows % (16 * CHUNKS) == 0
+        and strip_rows % (16 * LINKS) == 0
+        and strip_rows % 32 == 0
         and strip_rows % orbitals == 0
         and group_rows // orbitals == dyson_inverse.shape[2]
     )

time: 157 us -> 151 us (0.962)
  Pallas kernels: 156 us -> 149 us
    pallas_call x1, Pallas kernels: 150 us -> 143 us  [fused(): pl.pallas_call(functools.partial(fused_kernel, lines, rows, count, packed...]
where the time goes in v4:
time: 151 us; the launch traced here: 150 us
  Pallas kernels  149 us (99%)
    pallas_call x1, Pallas kernels, fused(): pl.pallas_call(functools.partial(fused_kernel, lines, rows, count, packed...  143 us
    pallas_call x1, Pallas kernels, widen(): pl.pallas_call(functools.partial(widen_kernel, pieces), out_shape=(jax.Sh...  6.18 us

profile of v4, /device:TPU:27, one launch (start us, length us, event | category | flops | bytes accessed | tf_op | source)
XLA Modules:
  0.0 149.5 jit_solution(15970816838553827672)
XLA Ops:
  0.6 142.7 %group_updates.1 = (f32[2,256,1024]{2,1,0:T(8,128)}, bf16[2,2048,512]{2,1,0:T(8,128)(2,1)}) custom-call(f32[2,256,1024]{2,1,0:T(8,128)} %strip.1, bf16[2,1024,512]{2,1,0:T(8,128)(2,1)} %history.1, f32[32]{0:T(128)} %coupling.1, f32[2,2,64,64]{3,2,1,0:T(8,128)} %inverse.1), custom_call_target="tpu_custom_call" | custom-call | tf_op jit(solution)/shard_map/group_updates/pallas_call | solution.py:712
  143.3 6.2 %widen.1 = (f32[2,2048,512]{2,1,0:T(8,128)}, f32[2,256,1024]{2,1,0:T(8,128)}) custom-call(bf16[2,2048,512]{2,1,0:T(8,128)(2,1)} %get-tuple-element.4.wide, f32[2,256,1024]{2,1,0:T(8,128)} %get-tuple-element.5.later), custom_call_target="tpu_custom_call" | custom-call | tf_op jit(solution)/shard_map/widen/pallas_call | solution.py:793
